TPU v7x, 256 devices: a whole 4x4x8 slice. The times are simulated.
256 devices in a mesh: row: 16 (over z_hi, x), col: 16 (over y, z_lo, core).
Axes of the slice: x: 4, y: 4, z: 8 (z_hi: 4, z_lo: 2; z = z_hi * 2 + z_lo), core: 2. Of those that a mesh axis runs over, the one named last changes fastest.
Arguments:
- queries: bfloat16 [16, 768, 768], P('row', 'col'), may hold values from -18 to 18
- keys: bfloat16 [16, 768, 768], P('col', 'row'), may hold values from -18 to 18
Outputs:
- grad_queries: float32 [16, 768, 768], P('row', 'col')
- grad_keys: float32 [16, 768, 768], P('col', 'row')
All inputs are finite; a program needn't handle non-finite values.
Results may differ from a plain program's by a relative error of at most 0.005.
Values may be sent and summed in bfloat16 or wider, within the bound.
A program may use at most 64 MiB of HBM per device.

v0:
```python
import jax
import jax.numpy as jnp
from jax import lax
from jax.sharding import PartitionSpec as P


def contract(left_side, right_side, left_dim, right_dim):
    return lax.dot_general(
        left_side,
        right_side,
        (((left_dim,), (right_dim,)), ((), ())),
        preferred_element_type=jnp.float32,
    )


def cycle_terms(query_frame, key_frame, score_scale, frames):
    scores = score_scale * contract(query_frame, key_frame, 1, 1)
    by_rows = jax.nn.softmax(scores, axis=1)
    by_cols = jax.nn.softmax(scores, axis=0)
    rows_half = by_rows.astype(jnp.bfloat16)
    cols_half = by_cols.astype(jnp.bfloat16)
    warped = contract(cols_half, query_frame, 0, 0).astype(jnp.bfloat16)
    cycled = jnp.dot(rows_half, warped, preferred_element_type=jnp.float32)
    residual = (cycled - query_frame.astype(jnp.float32)) / frames
    resid_half = residual.astype(jnp.bfloat16)
    grad_rows = contract(resid_half, warped, 1, 1)
    grad_warp = contract(rows_half, resid_half, 0, 0).astype(jnp.bfloat16)
    grad_cols = contract(query_frame, grad_warp, 1, 1)
    grad_scores = by_rows * (grad_rows - jnp.sum(grad_rows * by_rows, axis=1, keepdims=True))
    grad_scores = grad_scores + by_cols * (
        grad_cols - jnp.sum(grad_cols * by_cols, axis=0, keepdims=True)
    )
    score_half = (score_scale * grad_scores).astype(jnp.bfloat16)
    return (cols_half, grad_warp, score_half, residual)


def local(queries, keys):
    whole_q = lax.all_gather(queries, "col", axis=1, tiled=True)
    whole_k = lax.all_gather(keys, "row", axis=1, tiled=True)
    source_count = whole_q.shape[0]
    target_count = whole_k.shape[0]
    feature_width = whole_q.shape[2]
    frames = source_count * lax.axis_size("row")
    score_scale = feature_width ** (-0.5)
    pair_count = source_count * target_count
    empty_k = jnp.zeros(whole_k.shape, jnp.float32)

    def frames_of(pair_index):
        source_at = pair_index // target_count
        target_at = pair_index % target_count
        query_frame = lax.dynamic_index_in_dim(whole_q, source_at, 0, False)
        key_frame = lax.dynamic_index_in_dim(whole_k, target_at, 0, False)
        return (source_at, target_at, query_frame, key_frame)

    def add_pair(pair_index, totals):
        grad_q, grad_k = totals
        source_at, target_at, query_frame, key_frame = frames_of(pair_index)
        cols_half, grad_warp, score_half, residual = cycle_terms(
            query_frame, key_frame, score_scale, frames
        )
        q_term = jnp.dot(cols_half, grad_warp, preferred_element_type=jnp.float32)
        q_term = (
            q_term + jnp.dot(score_half, key_frame, preferred_element_type=jnp.float32) - residual
        )
        k_term = contract(score_half, query_frame, 0, 0)
        return (grad_q.at[source_at].add(q_term), grad_k.at[target_at].add(k_term))

    empty_q = jnp.zeros(whole_q.shape, jnp.float32)
    grad_q, grad_k = lax.fori_loop(0, pair_count, add_pair, (empty_q, empty_k))
    out_q = lax.psum_scatter(grad_q, "col", scatter_dimension=1, tiled=True)
    out_k = lax.psum_scatter(grad_k, "row", scatter_dimension=1, tiled=True)
    return (out_q, out_k)


def solution(mesh):
    placed = (P("row", "col", None), P("col", "row", None))
    return jax.shard_map(
        local,
        mesh=mesh,
        in_specs=placed,
        out_specs=(P("row", "col", None), P("col", "row", None)),
        check_vma=False,
    )
```

profile of v0, /device:TPU:1, one launch (start us, length us, event | category | flops | bytes accessed | tf_op | source)
XLA Modules:
  0.0 291.3 jit_solution(1062512941428547320)
XLA Ops:
  7.2 0.0 all-gather.3.cloned.1.call-start
  7.2 0.7 all-gather.3.cloned.1.call-update
  7.9 0.0 all-gather.5.cloned.1.call-start
  7.9 0.7 all-gather.5.cloned.1.call-update
  8.6 0.0 reduce-scatter.5.cloned.1.call-start
  8.7 40.3 %all-gather.3.cloned.1.call-done = bf16[1,768,768]{2,1,0:T(8,128)(2,1)} async-done(((bf16[1,48,768]{2,1,0:T(8,128)(2,1)}), bf16[1,768,768]{2,1,0:T(8,128)(2,1)}) %all-gather.3.cloned.1.call-update) | async-done | bytes 1179664 | tf_op jit(solution)/shard_map/all_gather | solution.py:38
  49.0 54.2 %all-gather.5.cloned.1.call-done = bf16[1,768,768]{2,1,0:T(8,128)(2,1)} async-done(((bf16[1,48,768]{2,1,0:T(8,128)(2,1)}), bf16[1,768,768]{2,1,0:T(8,128)(2,1)}) %all-gather.5.cloned.1.call-update) | async-done | bytes 1179664 | tf_op jit(solution)/shard_map/all_gather | solution.py:39
  103.2 2.8 fusion.29
  106.1 0.0 copy-start
  106.1 0.0 copy-start.5
  106.1 1.0 fusion.8
  107.1 1.1 copy-done.5
  108.2 2.6 fusion.15
  110.8 0.0 copy-done
  110.8 5.4 %online-softmax = f32[768,768]{1,0:T(8,128)} custom-call(f32[768,768]{1,0:T(8,128)} %copy-done, f32[768,768]{1,0:T(8,128)} %fusion.15), custom_call_target="tpu_custom_call" | custom-call | tf_op online-softmax
  116.2 3.9 %convolution_convert_fusion = bf16[768,768]{1,0:T(8,128)(2,1)S(1)} fusion(f32[768,768]{1,0:T(8,128)} %online-softmax, bf16[1,768,768]{2,1,0:T(8,128)(2,1)S(1)} %copy-done.5, f32[768,768]{1,0:T(8,128)} %copy-done, f32[768]{0:T(1024)S(1)} %get-tuple-element.56, f32[768]{0:T(1024)S(1)} %get-tuple-element.58), kind=kOutput, calls=%fused_computation.18 | convolution fusion | flops 910688256 | bytes 7084032 | tf_op jit(solution)/shard_map/while/body/eval_jaxpr/dot_general | solution.py:8
  120.1 0.0 copy-start.9
  120.1 1.0 copy-done.9
  121.1 0.0 copy-start.1
  121.1 0.0 copy-start.2
  121.1 0.0 copy-start.4
  121.1 1.1 fusion.13
  122.2 0.5 copy-done.1
  122.8 0.7 copy-done.2
  123.5 0.7 copy-done.4
  124.2 1.7 multiply_reduce_fusion
  125.9 0.0 copy-start.6
  125.9 1.5 fusion.4
  127.4 0.0 copy-done.6
  127.4 2.5 convolution_bitcast_fusion
  129.9 0.0 reduce-scatter.5.cloned.1.call-update
  130.0 0.0 reduce-scatter.3.cloned.1.call-start
  130.0 0.0 copy-start.3
  130.0 0.0 copy-start.7
  130.0 0.0 copy-start.8
  130.0 2.6 fusion.21
  132.6 0.0 copy-done.3
  132.7 0.0 copy-done.7
  132.7 0.0 copy-done.8
  132.7 2.6 subtract_bitcast_fusion
  135.3 0.0 reduce-scatter.3.cloned.1.call-update
  135.4 82.0 %reduce-scatter.5.cloned.1.call-done = f32[1,48,768]{2,1,0:T(8,128)} async-done(((f32[1,768,768]{2,1,0:T(8,128)}), f32[1,48,768]{2,1,0:T(8,128)}) %reduce-scatter.5.cloned.1.call-update) | async-done | bytes 147472 | tf_op jit(solution)/shard_map/reduce_scatter | solution.py:71
  217.3 67.4 %reduce-scatter.3.cloned.1.call-done = f32[1,48,768]{2,1,0:T(8,128)} async-done(((f32[1,768,768]{2,1,0:T(8,128)}), f32[1,48,768]{2,1,0:T(8,128)}) %reduce-scatter.3.cloned.1.call-update) | async-done | bytes 147472 | tf_op jit(solution)/shard_map/reduce_scatter | solution.py:70
Async XLA Ops:
  7.2 41.8 %all-gather.3.cloned.1.call-start = ((), (), s32[]{:S(2)}) async-start(), calls=%async_computation.2 | async-start | bytes 1253376 | tf_op jit(solution)/shard_map/all_gather | solution.py:38
  7.9 95.3 %all-gather.5.cloned.1.call-start = ((), (), s32[]{:S(2)}) async-start(), calls=%async_computation.3 | async-start | bytes 1253376 | tf_op jit(solution)/shard_map/all_gather | solution.py:39
  8.6 208.7 %reduce-scatter.5.cloned.1.call-start = ((), (), s32[]{:S(2)}) async-start(), calls=%async_computation.5 | async-start | bytes 2506752 | tf_op jit(solution)/shard_map/reduce_scatter | solution.py:71
  106.1 4.7 %copy-start = (f32[768,768]{1,0:T(8,128)}, f32[768,768]{1,0:T(8,128)S(1)}, u32[]{:S(2)}) copy-start(f32[768,768]{1,0:T(8,128)S(1)} %get-tuple-element.60) | copy-start | bytes 7077892
  106.1 2.1 copy-start.5
  120.1 1.0 copy-start.9
  121.1 1.7 copy-start.1
  121.1 2.4 copy-start.2
  121.1 3.1 %copy-start.4 = (f32[768,768]{1,0:T(8,128)S(1)}, f32[768,768]{1,0:T(8,128)}, u32[]{:S(2)}) copy-start(f32[768,768]{1,0:T(8,128)} %fusion.15) | copy-start | bytes 7077892
  125.9 1.5 copy-start.6
  130.0 154.8 %reduce-scatter.3.cloned.1.call-start = ((), (), s32[]{:S(2)}) async-start(), calls=%async_computation.4 | async-start | bytes 2506752 | tf_op jit(solution)/shard_map/reduce_scatter | solution.py:70
  130.0 2.6 copy-start.3
  130.0 2.6 copy-start.7
  130.0 2.7 copy-start.8
Sparse Core Ops, SparseCore 0:
  9.8 39.1 all-gather.2
  51.4 51.7 all-gather.4
  130.1 87.2 reduce-scatter.4
  220.3 64.3 reduce-scatter.2
where the time goes:
time: 294 us; the launch traced here: 291 us
  waiting for transfers between devices  245 us (83%)
  matrix products  19.9 us (7%)
  between operations  13.9 us (5%)
  Pallas kernels  5.36 us (2%)
  local copies, waits for them, and re-layouts  4.1 us (1%)
    reduce_scatter x1, waiting for transfers between devices, local(): out_k = lax.psum_scatter(grad_k, 'row', scatter_dimension=1, tiled=True)  82 us
    reduce_scatter x1, waiting for transfers between devices, local(): out_q = lax.psum_scatter(grad_q, 'col', scatter_dimension=1, tiled=True)  67.4 us
    all_gather x1, waiting for transfers between devices, local(): whole_k = lax.all_gather(keys, 'row', axis=1, tiled=True)  54.2 us
    all_gather x1, waiting for transfers between devices, local(): whole_q = lax.all_gather(queries, 'col', axis=1, tiled=True)  40.3 us
    dot_general x6, matrix products, contract(): lax.dot_general(left_side, right_side, (((left_dim,), (right_dim,)), ((),...  14.7 us
  transfers between devices with their start and end apart: 4, of which 4 were waited for; matrix products, arithmetic and copies ran while one was open for 2% of the time, Pallas kernels for 0%

commit v1 on v0

v1 whole, which is shorter than its diff:
```python
import jax
import jax.numpy as jnp
from jax import lax
from jax.experimental import pallas as pl
from jax.experimental.pallas import tpu as pltpu
from jax.sharding import PartitionSpec as P

MESH = pl.DeviceIdType.MESH
BF16 = jnp.bfloat16
F32 = jnp.float32


def contract(left_side, right_side, left_dim, right_dim):
    return lax.dot_general(
        left_side,
        right_side,
        (((left_dim,), (right_dim,)), ((), ())),
        preferred_element_type=jnp.float32,
    )


def cycle_terms(query_frame, key_frame, score_scale, frames):
    scores = score_scale * contract(query_frame, key_frame, 1, 1)
    by_rows = jax.nn.softmax(scores, axis=1)
    by_cols = jax.nn.softmax(scores, axis=0)
    rows_half = by_rows.astype(jnp.bfloat16)
    cols_half = by_cols.astype(jnp.bfloat16)
    warped = contract(cols_half, query_frame, 0, 0).astype(jnp.bfloat16)
    cycled = jnp.dot(rows_half, warped, preferred_element_type=jnp.float32)
    residual = (cycled - query_frame.astype(jnp.float32)) / frames
    resid_half = residual.astype(jnp.bfloat16)
    grad_rows = contract(resid_half, warped, 1, 1)
    grad_warp = contract(rows_half, resid_half, 0, 0).astype(jnp.bfloat16)
    grad_cols = contract(query_frame, grad_warp, 1, 1)
    grad_scores = by_rows * (grad_rows - jnp.sum(grad_rows * by_rows, axis=1, keepdims=True))
    grad_scores = grad_scores + by_cols * (
        grad_cols - jnp.sum(grad_cols * by_cols, axis=0, keepdims=True)
    )
    score_half = (score_scale * grad_scores).astype(jnp.bfloat16)
    return (cols_half, grad_warp, score_half, residual)


class Place:
    def __init__(self):
        row = lax.axis_index("row")
        col = lax.axis_index("col")
        self.zh, self.x = row // 4, row % 4
        self.y, self.zl, self.c = col // 4, (col // 2) % 2, col % 2
        self.row, self.col = row, col

    def at_x(self, step):
        return (self.zh * 4 + (self.x + step + 4) % 4, self.col)

    def at_zh(self, step):
        return (((self.zh + step + 4) % 4) * 4 + self.x, self.col)

    def at_y(self, step):
        return (self.row, ((self.y + step + 4) % 4) * 4 + self.zl * 2 + self.c)

    def at_zl(self):
        return (self.row, self.y * 4 + (1 - self.zl) * 2 + self.c)

    def at_core(self):
        return (self.row, self.y * 4 + self.zl * 2 + 1 - self.c)


def greet(at):
    barrier = pltpu.get_barrier_semaphore()
    for other in (
        at.at_core(),
        at.at_zl(),
        at.at_x(1),
        at.at_x(-1),
        at.at_y(1),
        at.at_y(-1),
        at.at_zh(1),
        at.at_zh(-1),
    ):
        pl.semaphore_signal(barrier, inc=1, device_id=other, device_id_type=MESH)
    pl.semaphore_wait(barrier, 8)


class Sends:
    def __init__(self, send_sem):
        self.send_sem = send_sem
        self.started = []

    def go(self, src, dst, recv, device):
        copy = pltpu.make_async_remote_copy(
            src_ref=src,
            dst_ref=dst,
            send_sem=self.send_sem.at[len(self.started)],
            recv_sem=recv,
            device_id=device,
            device_id_type=MESH,
        )
        copy.start()
        self.started.append(copy)

    def finish(self):
        for copy in self.started:
            copy.wait_send()


def kslot(dx, dz):
    return (dx % 4) * 4 + dz % 4


def qslot(dy, dzl, dc):
    return ((dy % 4) * 2 + dzl) * 2 + dc


def gather_kernel(q_ref, k_ref, qf, kf, send_sem, q_sem, k_sem):
    at = Place()
    s = 1 - 2 * at.c
    low = 3 - 2 * at.c
    high = 1 + 2 * at.c
    greet(at)
    out = Sends(send_sem)

    def got_k(dx, dz):
        slot = kslot(dx, dz)
        pltpu.make_async_remote_copy(
            src_ref=kf.at[slot], dst_ref=kf.at[slot], send_sem=send_sem.at[0],
            recv_sem=k_sem.at[slot], device_id=at.at_core(), device_id_type=MESH,
        ).wait_recv()

    def got_q(dy, dzl, dc):
        slot = qslot(dy, dzl, dc)
        pltpu.make_async_remote_copy(
            src_ref=qf.at[slot], dst_ref=qf.at[slot], send_sem=send_sem.at[0],
            recv_sem=q_sem.at[slot], device_id=at.at_core(), device_id_type=MESH,
        ).wait_recv()

    def send_k(src, slot, device):
        out.go(src, kf.at[slot], k_sem.at[slot], device)

    def send_q(src, slot, device):
        out.go(src, qf.at[slot], q_sem.at[slot], device)

    def k_along_x(src, dz):
        send_k(src, kslot(3, dz), at.at_x(1))
        send_k(src, kslot(1, dz), at.at_x(-1))

    def k_relay_x(dz):
        if dz % 2 == 0:
            send_k(kf.at[low * 4 + dz], kslot(2, dz), at.at_x(s))
        else:
            send_k(kf.at[high * 4 + dz], kslot(2, dz), at.at_x(-s))

    def q_along_y(src, dzl):
        send_q(src, qslot(3, dzl, 0), at.at_y(1))
        send_q(src, qslot(1, dzl, 0), at.at_y(-1))

    def q_relay_y(dzl):
        if dzl == 0:
            send_q(qf.at[low * 4 + dzl * 2], qslot(2, dzl, 0), at.at_y(s))
        else:
            send_q(qf.at[high * 4 + dzl * 2], qslot(2, dzl, 0), at.at_y(-s))

    def q_to_core(src, dy, dzl):
        send_q(src, qslot(dy, dzl, 1), at.at_core())

    send_q(q_ref, qslot(0, 1, 0), at.at_zl())
    send_k(k_ref, kslot(0, 3), at.at_zh(1))
    send_k(k_ref, kslot(0, 1), at.at_zh(-1))
    k_along_x(k_ref, 0)
    q_along_y(q_ref, 0)
    q_to_core(q_ref, 0, 0)
    kf[kslot(0, 0)] = k_ref[...]
    qf[qslot(0, 0, 0)] = q_ref[...]

    got_q(0, 1, 0)
    q_along_y(qf.at[qslot(0, 1, 0)], 1)
    q_to_core(qf.at[qslot(0, 1, 0)], 0, 1)

    got_k(3, 0)
    got_k(1, 0)
    k_relay_x(0)

    got_q(3, 0, 0)
    got_q(1, 0, 0)
    q_relay_y(0)
    q_to_core(qf.at[qslot(3, 0, 0)], 3, 0)
    q_to_core(qf.at[qslot(1, 0, 0)], 1, 0)

    got_k(0, 3)
    got_k(0, 1)
    send_k(kf.at[low], kslot(0, 2), at.at_zh(s))
    k_along_x(kf.at[kslot(0, 1)], 1)
    k_along_x(kf.at[kslot(0, 3)], 3)

    got_q(3, 1, 0)
    got_q(1, 1, 0)
    q_relay_y(1)
    q_to_core(qf.at[qslot(3, 1, 0)], 3, 1)
    q_to_core(qf.at[qslot(1, 1, 0)], 1, 1)

    got_q(2, 0, 0)
    q_to_core(qf.at[qslot(2, 0, 0)], 2, 0)

    got_k(0, 2)
    k_along_x(kf.at[kslot(0, 2)], 2)

    got_q(2, 1, 0)
    q_to_core(qf.at[qslot(2, 1, 0)], 2, 1)

    for dz in (1, 3):
        got_k(3, dz)
        got_k(1, dz)
        k_relay_x(dz)
    got_k(3, 2)
    got_k(1, 2)
    k_relay_x(2)

    for dz in (0, 1, 3, 2):
        got_k(2, dz)
    for dy in (0, 1, 3, 2):
        for dzl in (0, 1):
            got_q(dy, dzl, 1)
    out.finish()


def gather(queries, keys):
    rows, width = queries.shape
    full = jax.ShapeDtypeStruct((16, rows, width), BF16)
    vmem = pl.BlockSpec(memory_space=pltpu.VMEM)
    return pl.pallas_call(
        gather_kernel,
        out_shape=(full, full),
        in_specs=[vmem, vmem],
        out_specs=(vmem, vmem),
        scratch_shapes=[
            pltpu.SemaphoreType.DMA((32,)),
            pltpu.SemaphoreType.DMA((16,)),
            pltpu.SemaphoreType.DMA((16,)),
        ],
        compiler_params=pltpu.CompilerParams(
            collective_id=0, has_side_effects=True, vmem_limit_bytes=32 * 2**20
        ),
        name="gather_frames",
    )(queries, keys)


def reduce_kernel(
    qp, kp, q_out, k_out,
    kstage, kopp, kin, kzst, kzopp, kzin,
    qcst, qcin, qsum, qstage, qopp, qin, qzst, qzin,
    send_sem, kopp_sem, kin_sem, kz_sem, qc_sem, qopp_sem, qin_sem, qz_sem,
):
    at = Place()
    s = 1 - 2 * at.c
    low = 3 - 2 * at.c
    high = 1 + 2 * at.c
    greet(at)
    out = Sends(send_sem)

    def got(ref, sem):
        pltpu.make_async_remote_copy(
            src_ref=ref, dst_ref=ref, send_sem=send_sem.at[0],
            recv_sem=sem, device_id=at.at_core(), device_id_type=MESH,
        ).wait_recv()

    for dy in (2, 1, 3, 0):
        for dzl in (1, 0):
            slot = dy * 2 + dzl
            qcst[slot] = qp[qslot(dy, dzl, 1)].astype(BF16)
            out.go(qcst.at[slot], qcin.at[slot], qc_sem.at[slot], at.at_core())

    for dz in (2, 1, 3, 0):
        kstage[kslot(2, dz)] = kp[kslot(2, dz)].astype(BF16)
        out.go(kstage.at[kslot(2, dz)], kopp.at[dz], kopp_sem.at[dz], at.at_x(s if dz % 2 == 0 else -s))
    for dz in (2, 1, 3, 0):
        if dz % 2 == 0:
            slot = low * 4 + dz
            kstage[slot] = kp[slot].astype(BF16)
            out.go(kstage.at[slot], kin.at[4 + dz], kin_sem.at[4 + dz], at.at_x(-s))
        else:
            slot = high * 4 + dz
            kstage[slot] = kp[slot].astype(BF16)
            out.go(kstage.at[slot], kin.at[dz], kin_sem.at[dz], at.at_x(s))

    def core_sum(dy, dzl):
        slot = dy * 2 + dzl
        got(qcin.at[slot], qc_sem.at[slot])
        qsum[slot] = qp[qslot(dy, dzl, 0)] + qcin[slot].astype(F32)

    for dzl in (1, 0):
        core_sum(2, dzl)
        slot = 4 + dzl
        qstage[slot] = qsum[slot].astype(BF16)
        out.go(qstage.at[slot], qopp.at[dzl], qopp_sem.at[dzl], at.at_y(s if dzl == 0 else -s))
    for dy in (1, 3):
        for dzl in (1, 0):
            core_sum(dy, dzl)
    slot = high * 2 + 1
    qstage[slot] = qsum[slot].astype(BF16)
    out.go(qstage.at[slot], qin.at[1], qin_sem.at[1], at.at_y(s))
    slot = low * 2
    qstage[slot] = qsum[slot].astype(BF16)
    out.go(qstage.at[slot], qin.at[2], qin_sem.at[2], at.at_y(-s))

    for dz in (2, 1, 3, 0):
        got(kopp.at[dz], kopp_sem.at[dz])
        if dz % 2 == 0:
            slot = high * 4 + dz
            kstage[slot] = (kp[slot] + kopp[dz].astype(F32)).astype(BF16)
            out.go(kstage.at[slot], kin.at[dz], kin_sem.at[dz], at.at_x(s))
        else:
            slot = low * 4 + dz
            kstage[slot] = (kp[slot] + kopp[dz].astype(F32)).astype(BF16)
            out.go(kstage.at[slot], kin.at[4 + dz], kin_sem.at[4 + dz], at.at_x(-s))

    got(qopp.at[1], qopp_sem.at[1])
    slot = low * 2 + 1
    qstage[slot] = (qsum[slot] + qopp[1].astype(F32)).astype(BF16)
    out.go(qstage.at[slot], qin.at[3], qin_sem.at[3], at.at_y(-s))
    got(qopp.at[0], qopp_sem.at[0])
    slot = high * 2
    qstage[slot] = (qsum[slot] + qopp[0].astype(F32)).astype(BF16)
    out.go(qstage.at[slot], qin.at[0], qin_sem.at[0], at.at_y(s))

    core_sum(0, 1)
    core_sum(0, 0)
    got(qin.at[1], qin_sem.at[1])
    got(qin.at[3], qin_sem.at[3])
    qzst[...] = (qsum[1] + qin[1].astype(F32) + qin[3].astype(F32)).astype(BF16)
    out.go(qzst, qzin, qz_sem.at[0], at.at_zl())

    def k_sum(slot, dz):
        return kp[slot] + kin[dz].astype(F32) + kin[4 + dz].astype(F32)

    def k_ready(dz):
        got(kin.at[dz], kin_sem.at[dz])
        got(kin.at[4 + dz], kin_sem.at[4 + dz])

    k_ready(2)
    kzst[2] = k_sum(2, 2).astype(BF16)
    out.go(kzst.at[2], kzopp, kz_sem.at[2], at.at_zh(s))
    k_ready(1)
    k_ready(3)
    kzst[1] = k_sum(low, low).astype(BF16)
    out.go(kzst.at[1], kzin.at[1], kz_sem.at[1], at.at_zh(-s))
    ahead = k_sum(high, high)
    got(kzopp, kz_sem.at[2])
    kzst[0] = (ahead + kzopp[...].astype(F32)).astype(BF16)
    out.go(kzst.at[0], kzin.at[0], kz_sem.at[0], at.at_zh(s))

    got(qin.at[0], qin_sem.at[0])
    got(qin.at[2], qin_sem.at[2])
    got(qzin, qz_sem.at[0])
    q_out[...] = (qsum[0] + qin[0].astype(F32) + qin[2].astype(F32)) + qzin[...].astype(F32)

    k_ready(0)
    total = k_sum(0, 0)
    got(kzin.at[0], kz_sem.at[0])
    got(kzin.at[1], kz_sem.at[1])
    k_out[...] = total + kzin[0].astype(F32) + kzin[1].astype(F32)
    out.finish()


def reduce_scatter(q_terms, k_terms):
    _, rows, width = q_terms.shape
    vmem = pl.BlockSpec(memory_space=pltpu.VMEM)
    own = jax.ShapeDtypeStruct((rows, width), F32)

    def buf(*lead, dtype=BF16):
        return pltpu.VMEM((*lead, rows, width), dtype)

    def sems(count):
        return pltpu.SemaphoreType.DMA((count,))

    return pl.pallas_call(
        reduce_kernel,
        out_shape=(own, own),
        in_specs=[vmem, vmem],
        out_specs=(vmem, vmem),
        scratch_shapes=[
            buf(16), buf(4), buf(8), buf(3), buf(), buf(2),
            buf(8), buf(8), buf(8, dtype=F32), buf(8), buf(2), buf(4), buf(), buf(),
            sems(32), sems(4), sems(8), sems(3), sems(8), sems(2), sems(4), sems(1),
        ],
        compiler_params=pltpu.CompilerParams(
            collective_id=1, has_side_effects=True, vmem_limit_bytes=48 * 2**20
        ),
        name="reduce_terms",
    )(q_terms, k_terms)


def local(queries, keys):
    frames = queries.shape[0] * lax.axis_size("row")
    _, rows, width = queries.shape
    whole_q, whole_k = gather(queries[0], keys[0])
    query_frame = whole_q.reshape(16 * rows, width)
    key_frame = whole_k.reshape(16 * rows, width)
    cols_half, grad_warp, score_half, residual = cycle_terms(
        query_frame, key_frame, width**-0.5, frames
    )
    q_term = jnp.dot(cols_half, grad_warp, preferred_element_type=jnp.float32)
    q_term = q_term + jnp.dot(score_half, key_frame, preferred_element_type=jnp.float32) - residual
    k_term = contract(score_half, query_frame, 0, 0)
    out_q, out_k = reduce_scatter(q_term.reshape(16, rows, width), k_term.reshape(16, rows, width))
    return (out_q[None], out_k[None])


def solution(mesh):
    placed = (P("row", "col", None), P("col", "row", None))
    return jax.shard_map(
        local,
        mesh=mesh,
        in_specs=placed,
        out_specs=(P("row", "col", None), P("col", "row", None)),
        check_vma=False,
    )
```

time: 294 us -> 82.2 us (0.28)
  the two profiles are of different devices: /device:TPU:1 before, /device:TPU:8 now
where the time goes in v1:
time: 82.2 us; the launch traced here: 81.9 us
  Pallas kernels  56 us (68%)
  matrix products  12.9 us (16%)
  local copies, waits for them, and re-layouts  7.52 us (9%)
  other arithmetic  4.81 us (6%)
    pallas_call x1, Pallas kernels, gather(): pl.pallas_call(gather_kernel, out_shape=(full, full), in_specs=[vmem, vme...  27 us
    pallas_call x1, Pallas kernels, reduce_scatter(): pl.pallas_call(reduce_kernel, out_shape=(own, own), in_specs=[vmem, vmem]...  23.6 us
    dot_general x6, matrix products, contract(): lax.dot_general(left_side, right_side, (((left_dim,), (right_dim,)), ((),...  10.4 us
    unnamed x1, Pallas kernels  5.36 us
    unnamed x20, local copies, waits for them, and re-layouts  5.15 us
    convert_element_type x1, local copies, waits for them, and re-layouts, cycle_terms(): score_half = (score_scale * grad_scores).astype(jnp.bfloat16)  2.37 us
    convert_element_type x1, other arithmetic, cycle_terms(): resid_half = residual.astype(jnp.bfloat16)  2.1 us
    convert_element_type x1, other arithmetic, cycle_terms(): score_half = (score_scale * grad_scores).astype(jnp.bfloat16)  1.71 us

profile of v1, /device:TPU:8, one launch (start us, length us, event | category | flops | bytes accessed | tf_op | source)
XLA Modules:
  0.0 81.9 jit_solution(10471989675499599587)
XLA Ops:
  0.6 0.0 copy-start.2
  0.6 0.9 %copy-done.2 = bf16[1,48,768]{2,1,0:T(8,128)(2,1)S(1)} copy-done((bf16[1,48,768]{2,1,0:T(8,128)(2,1)S(1)}, bf16[1,48,768]{2,1,0:T(8,128)(2,1)}, u32[]{:S(2)}) %copy-start.2) | copy-done | bytes 73752
  1.5 0.0 copy-start.3
  1.5 0.9 %copy-done.3 = bf16[1,48,768]{2,1,0:T(8,128)(2,1)S(1)} copy-done((bf16[1,48,768]{2,1,0:T(8,128)(2,1)S(1)}, bf16[1,48,768]{2,1,0:T(8,128)(2,1)}, u32[]{:S(2)}) %copy-start.3) | copy-done | bytes 73752
  2.4 27.0 %gather_frames.1 = (bf16[16,48,768]{2,1,0:T(8,128)(2,1)S(1)}, bf16[16,48,768]{2,1,0:T(8,128)(2,1)S(1)}) custom-call(bf16[48,768]{1,0:T(8,128)(2,1)S(1)} %bitcast.34, bf16[48,768]{1,0:T(8,128)(2,1)S(1)} %bitcast.35), custom_call_target="tpu_custom_call" | custom-call | tf_op jit(solution)/shard_map/gather_frames/pallas_call | solution.py:228
  29.4 0.0 copy-start
  29.4 1.2 %fusion.15 = (f32[768]{0:T(1024)S(1)}, f32[768]{0:T(1024)S(1)}, f32[768,768]{1,0:T(8,128)S(1)}) fusion(bf16[768,768]{1,0:T(8,128)(2,1)S(1)} %bitcast.25, bf16[768,768]{1,0:T(8,128)(2,1)S(1)} %bitcast.30), kind=kOutput, calls=%fused_computation.21 | convolution fusion | flops 907737600 | bytes 4724736 | tf_op jit(solution)/shard_map/dot_general | solution.py:14
  30.6 0.0 copy-done
  30.6 0.0 copy-start.4
  30.6 1.0 %fusion.3 = (f32[768]{0:T(1024)S(1)}, f32[768]{0:T(1024)S(1)}) fusion(f32[768,768]{1,0:T(8,128)S(1)} %get-tuple-element.16, f32[768]{0:T(1024)S(1)} %get-tuple-element.14, f32[768]{0:T(1024)S(1)} %get-tuple-element.15), kind=kLoop, calls=%fused_computation.10 | loop fusion | flops 2357760 | bytes 2371584 | tf_op jit(solution)/shard_map/reduce_sum | solution.py:24
  31.6 2.6 %fusion.10 = f32[768,768]{1,0:T(8,128)} fusion(bf16[768,768]{1,0:T(8,128)(2,1)S(1)} %bitcast.26, f32[768,768]{1,0:T(8,128)S(1)} %get-tuple-element.16, f32[768]{0:T(1024)S(1)} %get-tuple-element.13, f32[768]{0:T(1024)S(1)} %get-tuple-element.15), kind=kOutput, calls=%fused_computation.19 | convolution fusion | flops 907739136 | bytes 5904384 | tf_op jit(solution)/shard_map/dot_general | solution.py:14
  34.2 0.0 copy-done.4
  34.2 5.4 %online-softmax = f32[768,768]{1,0:T(8,128)} custom-call(f32[768,768]{1,0:T(8,128)} %copy-done.4, f32[768,768]{1,0:T(8,128)} %fusion.10), custom_call_target="tpu_custom_call" | custom-call | tf_op online-softmax
  39.5 0.0 copy-start.5
  39.6 2.1 %fusion.4 = bf16[768,768]{1,0:T(8,128)(2,1)S(1)} fusion(f32[768,768]{1,0:T(8,128)} %online-softmax, bf16[16,48,768]{2,1,0:T(8,128)(2,1)S(1)} %get-tuple-element.6), kind=kLoop, calls=%fused_computation.13 | loop fusion | flops 2359296 | bytes 4718592 | tf_op jit(solution)/shard_map/convert_element_type | solution.py:31
  41.7 0.3 copy-done.5
  41.9 1.6 %convolution_convert_fusion = bf16[768,768]{1,0:T(8,128)(2,1)S(1)} fusion(bf16[768,768]{1,0:T(8,128)(2,1)S(1)} %fusion.4, f32[768,768]{1,0:T(8,128)S(1)} %copy-done.5, f32[768]{0:T(1024)S(1)} %get-tuple-element.12, f32[768]{0:T(1024)S(1)} %get-tuple-element.14), kind=kOutput, calls=%fused_computation.12 | convolution fusion | flops 908328960 | bytes 4724736 | tf_op jit(solution)/shard_map/dot_general | solution.py:14
  43.5 0.0 copy-start.8
  43.5 1.1 %fusion.16 = f32[768,768]{1,0:T(8,128)S(1)} fusion(bf16[768,768]{1,0:T(8,128)(2,1)S(1)} %bitcast.27, bf16[768,768]{1,0:T(8,128)(2,1)S(1)} %convolution_convert_fusion), kind=kOutput, calls=%fused_computation.22 | convolution fusion | flops 905969664 | bytes 4718592 | tf_op jit(solution)/shard_map/dot_general | solution.py:14
  44.6 0.5 copy-done.8
  45.2 1.6 %multiply_reduce_fusion.1 = (f32[768]{0:T(1024)S(1)}, f32[768]{0:T(1024)S(1)}, f32[768,768]{1,0:T(8,128)S(1)}) fusion(f32[768]{0:T(1024)S(1)} %get-tuple-element.12, f32[768,768]{1,0:T(8,128)S(1)} %copy-done.5, f32[768]{0:T(1024)S(1)} %get-tuple-element.14, f32[768,768]{1,0:T(8,128)S(1)} %fusion.16, f32[768]{0:T(1024)S(1)} %get-tuple-element.13, ...), kind=kOutput, calls=%fused_computation.3 | convolution fusion | flops 911276544 | bytes 10635264 | tf_op jit(solution)/shard_map/dot_general | solution.py:14
  46.8 1.7 %multiply_convert_fusion = bf16[768,768]{1,0:T(8,128)(2,1)S(1)} fusion(f32[768,768]{1,0:T(8,128)S(1)} %fusion.16, f32[768,768]{1,0:T(8,128)S(1)} %get-tuple-element.17, f32[768]{0:T(1024)S(1)} %get-tuple-element.11, f32[768]{0:T(1024)S(1)} %get-tuple-element.10, f32[768]{0:T(1024)S(1)} %get-tuple-element.13, f32[768,768]{1,0:T(8,128)S(1)} %copy-done.5, ...), kind=kLoop, calls=%fused_computation.1 | loop fusion | flops 6488064 | bytes 8275968 | tf_op jit(solution)/shard_map/convert_element_type | solution.py:39
  48.5 0.0 copy-start.7
  48.5 0.0 copy-start.1
  48.5 0.0 copy-start.6
  48.5 1.2 %fusion.8 = f32[768,768]{1,0:T(8,128)S(1)} fusion(bf16[768,768]{1,0:T(8,128)(2,1)S(1)} %convolution_convert_fusion, f32[768,768]{1,0:T(8,128)S(1)} %copy-done.5, f32[768]{0:T(1024)S(1)} %get-tuple-element.13, f32[768]{0:T(1024)S(1)} %get-tuple-element.15), kind=kOutput, calls=%fused_computation.17 | convolution fusion | flops 907739136 | bytes 5904384 | tf_op jit(solution)/shard_map/dot_general | solution.py:399
  49.7 0.0 copy-done.7
  49.7 0.5 copy-done.1
  50.2 0.7 copy-done.6
  51.0 1.3 %add_subtract_fusion = f32[768,768]{1,0:T(8,128)S(1)} fusion(f32[768,768]{1,0:T(8,128)S(1)} %fusion.8, bf16[768,768]{1,0:T(8,128)(2,1)S(1)} %multiply_convert_fusion, bf16[768,768]{1,0:T(8,128)(2,1)S(1)} %bitcast.31, f32[768,768]{1,0:T(8,128)S(1)} %copy-done.6, bf16[768,768]{1,0:T(8,128)(2,1)S(1)} %bitcast.28), kind=kOutput, calls=%fused_computation | convolution fusion | flops 908918784 | bytes 10616832 | tf_op jit(solution)/shard_map/dot_general | solution.py:400
  52.2 2.4 %copy.15 = bf16[768,768]{1,0:T(8,128)(2,1)} copy(bf16[768,768]{0,1:T(8,128)(2,1)} %bitcast.36) | data formatting | bytes 2359296 | tf_op jit(solution)/shard_map/convert_element_type | solution.py:39
  54.6 2.3 %fusion.17.kp = f32[16,48,768]{2,1,0:T(8,128)S(1)} fusion(bf16[16,48,768]{2,1,0:T(8,128)(2,1)} %bitcast.37, bf16[768,768,1]{1,0,2:T(8,128)(2,1)S(1)} %bitcast.29), kind=kOutput, calls=%fused_computation.23 | convolution fusion | flops 905969664 | bytes 4718592 | tf_op jit(solution)/shard_map/dot_general | solution.py:14
  56.9 23.6 %reduce_terms.1 = (f32[48,768]{1,0:T(8,128)S(1)}, f32[48,768]{1,0:T(8,128)S(1)}) custom-call(f32[16,48,768]{2,1,0:T(8,128)S(1)} %bitcast.24, f32[16,48,768]{2,1,0:T(8,128)S(1)} %fusion.17.kp), custom_call_target="tpu_custom_call" | custom-call | tf_op jit(solution)/shard_map/reduce_terms/pallas_call | solution.py:373
  80.6 0.7 copy.21
  81.3 0.7 copy.22
Async XLA Ops:
  0.6 0.9 %copy-start.2 = (bf16[1,48,768]{2,1,0:T(8,128)(2,1)S(1)}, bf16[1,48,768]{2,1,0:T(8,128)(2,1)}, u32[]{:S(2)}) copy-start(bf16[1,48,768]{2,1,0:T(8,128)(2,1)} %param.2) | copy-start | bytes 221188
  1.5 0.9 %copy-start.3 = (bf16[1,48,768]{2,1,0:T(8,128)(2,1)S(1)}, bf16[1,48,768]{2,1,0:T(8,128)(2,1)}, u32[]{:S(2)}) copy-start(bf16[1,48,768]{2,1,0:T(8,128)(2,1)} %param.3) | copy-start | bytes 221188
  29.4 1.2 %copy-start = (bf16[16,48,768]{2,1,0:T(8,128)(2,1)}, bf16[16,48,768]{2,1,0:T(8,128)(2,1)S(1)}, u32[]{:S(2)}) copy-start(bf16[16,48,768]{2,1,0:T(8,128)(2,1)S(1)} %get-tuple-element.7) | copy-start | bytes 3538948
  30.6 3.6 %copy-start.4 = (f32[768,768]{1,0:T(8,128)}, f32[768,768]{1,0:T(8,128)S(1)}, u32[]{:S(2)}) copy-start(f32[768,768]{1,0:T(8,128)S(1)} %get-tuple-element.16) | copy-start | bytes 7077892
  39.5 2.4 %copy-start.5 = (f32[768,768]{1,0:T(8,128)S(1)}, f32[768,768]{1,0:T(8,128)}, u32[]{:S(2)}) copy-start(f32[768,768]{1,0:T(8,128)} %copy-done.4) | copy-start | bytes 7077892
  43.5 1.7 %copy-start.8 = (f32[768,768]{1,0:T(8,128)S(1)}, f32[768,768]{1,0:T(8,128)}, u32[]{:S(2)}) copy-start(f32[768,768]{1,0:T(8,128)} %fusion.10) | copy-start | bytes 7077892
  48.5 1.2 %copy-start.7 = (bf16[768,768]{1,0:T(8,128)(2,1)}, bf16[768,768]{1,0:T(8,128)(2,1)S(1)}, u32[]{:S(2)}) copy-start(bf16[768,768]{1,0:T(8,128)(2,1)S(1)} %multiply_convert_fusion) | copy-start | bytes 3538948
  48.5 1.7 %copy-start.1 = (bf16[16,48,768]{2,1,0:T(8,128)(2,1)S(1)}, bf16[16,48,768]{2,1,0:T(8,128)(2,1)}, u32[]{:S(2)}) copy-start(bf16[16,48,768]{2,1,0:T(8,128)(2,1)} %copy-done) | copy-start | bytes 3538948
  48.5 2.4 %copy-start.6 = (f32[768,768]{1,0:T(8,128)S(1)}, f32[768,768]{1,0:T(8,128)}, u32[]{:S(2)}) copy-start(f32[768,768]{1,0:T(8,128)} %online-softmax) | copy-start | bytes 7077892

commit v2 on v1

v2 whole, which is shorter than its diff:
```python
import jax
import jax.numpy as jnp
from jax import lax
from jax.experimental import pallas as pl
from jax.experimental.pallas import tpu as pltpu
from jax.sharding import PartitionSpec as P

MESH = pl.DeviceIdType.MESH
BF16 = jnp.bfloat16
F32 = jnp.float32


def contract(left_side, right_side, left_dim, right_dim):
    return lax.dot_general(
        left_side,
        right_side,
        (((left_dim,), (right_dim,)), ((), ())),
        preferred_element_type=jnp.float32,
    )


def cycle_terms(query_frame, key_frame, score_scale, frames):
    scores = score_scale * contract(query_frame, key_frame, 1, 1)
    by_rows = jax.nn.softmax(scores, axis=1)
    by_cols = jax.nn.softmax(scores, axis=0)
    rows_half = by_rows.astype(jnp.bfloat16)
    cols_half = by_cols.astype(jnp.bfloat16)
    warped = contract(cols_half, query_frame, 0, 0).astype(jnp.bfloat16)
    cycled = jnp.dot(rows_half, warped, preferred_element_type=jnp.float32)
    residual = (cycled - query_frame.astype(jnp.float32)) / frames
    resid_half = residual.astype(jnp.bfloat16)
    grad_rows = contract(resid_half, warped, 1, 1)
    grad_warp = contract(rows_half, resid_half, 0, 0).astype(jnp.bfloat16)
    grad_cols = contract(query_frame, grad_warp, 1, 1)
    grad_scores = by_rows * (grad_rows - jnp.sum(grad_rows * by_rows, axis=1, keepdims=True))
    grad_scores = grad_scores + by_cols * (
        grad_cols - jnp.sum(grad_cols * by_cols, axis=0, keepdims=True)
    )
    score_half = (score_scale * grad_scores).astype(jnp.bfloat16)
    return (cols_half, grad_warp, score_half, residual)


class Place:
    def __init__(self):
        row = lax.axis_index("row")
        col = lax.axis_index("col")
        self.zh, self.x = row // 4, row % 4
        self.y, self.zl, self.c = col // 4, (col // 2) % 2, col % 2
        self.row, self.col = row, col

    def at_x(self, step):
        return (self.zh * 4 + (self.x + step + 4) % 4, self.col)

    def at_zh(self, step):
        return (((self.zh + step + 4) % 4) * 4 + self.x, self.col)

    def at_y(self, step):
        return (self.row, ((self.y + step + 4) % 4) * 4 + self.zl * 2 + self.c)

    def at_zl(self):
        return (self.row, self.y * 4 + (1 - self.zl) * 2 + self.c)

    def at_core(self):
        return (self.row, self.y * 4 + self.zl * 2 + 1 - self.c)


def greet(at):
    barrier = pltpu.get_barrier_semaphore()
    others = [at.at_core(), at.at_zl()]
    for step in (1, -1, 2):
        others += [at.at_x(step), at.at_y(step), at.at_zh(step)]
    for other in others:
        pl.semaphore_signal(barrier, inc=1, device_id=other, device_id_type=MESH)
    pl.semaphore_wait(barrier, len(others))


class Sends:
    def __init__(self, send_sem):
        self.send_sem = send_sem
        self.started = []

    def go(self, src, dst, recv, device):
        copy = pltpu.make_async_remote_copy(
            src_ref=src,
            dst_ref=dst,
            send_sem=self.send_sem.at[len(self.started)],
            recv_sem=recv,
            device_id=device,
            device_id_type=MESH,
        )
        copy.start()
        self.started.append(copy)

    def finish(self):
        for copy in self.started:
            copy.wait_send()


def kslot(dx, dz):
    return (dx % 4) * 4 + dz % 4


def qslot(dy, dzl, dc):
    return ((dy % 4) * 2 + dzl) * 2 + dc


def gather_kernel(q_ref, k_ref, qf, kf, send_sem, q_sem, k_sem):
    at = Place()
    greet(at)
    out = Sends(send_sem)

    def got(ref, sem):
        pltpu.make_async_remote_copy(
            src_ref=ref, dst_ref=ref, send_sem=send_sem.at[0],
            recv_sem=sem, device_id=at.at_core(), device_id_type=MESH,
        ).wait_recv()

    def got_k(dx, dz):
        slot = kslot(dx, dz)
        got(kf.at[slot], k_sem.at[slot])
        return kf.at[slot]

    def got_q(dy, dzl, dc):
        slot = qslot(dy, dzl, dc)
        got(qf.at[slot], q_sem.at[slot])
        return qf.at[slot]

    def k_along_x(src, dz, steps=(1, -1)):
        for step in steps:
            slot = kslot(-step, dz)
            out.go(src, kf.at[slot], k_sem.at[slot], at.at_x(step))

    def k_along_z(src, dx, steps=(1, -1)):
        for step in steps:
            slot = kslot(dx, -step)
            out.go(src, kf.at[slot], k_sem.at[slot], at.at_zh(step))

    def q_along_y(src, dzl):
        for step in (1, -1, 2):
            slot = qslot(-step, dzl, 0)
            out.go(src, qf.at[slot], q_sem.at[slot], at.at_y(step))

    def q_to_core(src, dy, dzl):
        slot = qslot(dy, dzl, 1)
        out.go(src, qf.at[slot], q_sem.at[slot], at.at_core())

    slot = qslot(0, 1, 0)
    out.go(q_ref, qf.at[slot], q_sem.at[slot], at.at_zl())
    k_along_z(k_ref, 0)
    k_along_x(k_ref, 0)
    q_along_y(q_ref, 0)
    k_along_z(k_ref, 0, (2,))
    k_along_x(k_ref, 0, (2,))
    q_to_core(q_ref, 0, 0)
    kf[kslot(0, 0)] = k_ref[...]
    qf[qslot(0, 0, 0)] = q_ref[...]

    block = got_q(0, 1, 0)
    q_along_y(block, 1)
    q_to_core(block, 0, 1)

    k_along_x(got_k(0, 1), 1)
    k_along_x(got_k(0, 3), 3)
    for dy in (1, 3, 2):
        q_to_core(got_q(dy, 0, 0), dy, 0)
    k_along_z(got_k(2, 0), 2)
    block = got_k(0, 2)
    k_along_x(block, 2)
    k_along_x(block, 2, (2,))
    for dy in (1, 3, 2):
        q_to_core(got_q(dy, 1, 0), dy, 1)

    for dx, dz in ((1, 0), (3, 0), (1, 1), (3, 1), (1, 3), (3, 3), (2, 1), (2, 3), (1, 2), (3, 2), (2, 2)):
        got_k(dx, dz)
    for dy in (0, 1, 3, 2):
        for dzl in (0, 1):
            got_q(dy, dzl, 1)
    out.finish()


def gather(queries, keys):
    rows, width = queries.shape
    full = jax.ShapeDtypeStruct((16, rows, width), BF16)
    vmem = pl.BlockSpec(memory_space=pltpu.VMEM)
    return pl.pallas_call(
        gather_kernel,
        out_shape=(full, full),
        in_specs=[vmem, vmem],
        out_specs=(vmem, vmem),
        scratch_shapes=[
            pltpu.SemaphoreType.DMA((32,)),
            pltpu.SemaphoreType.DMA((16,)),
            pltpu.SemaphoreType.DMA((16,)),
        ],
        compiler_params=pltpu.CompilerParams(
            collective_id=0, has_side_effects=True, vmem_limit_bytes=32 * 2**20
        ),
        name="gather_frames",
    )(queries, keys)


def reduce_kernel(
    qp, kp, q_out, k_out,
    kst, kx1, kx2, kzt, kzin, qcst, qcin, qsum, qst, qyin, qzst, qzin,
    send_sem, kx1_sem, kx2_sem, kzt_sem, kzin_sem, qc_sem, qy_sem, qz_sem,
):
    at = Place()
    greet(at)
    out = Sends(send_sem)

    def got(ref, sem):
        pltpu.make_async_remote_copy(
            src_ref=ref, dst_ref=ref, send_sem=send_sem.at[0],
            recv_sem=sem, device_id=at.at_core(), device_id_type=MESH,
        ).wait_recv()

    def send_k(dx, dz, dst, sem, device):
        slot = kslot(dx, dz)
        kst[slot] = kp[slot].astype(BF16)
        out.go(kst.at[slot], dst, sem, device)

    send_k(2, 1, kzt.at[0], kzt_sem.at[0], at.at_zh(1))
    send_k(2, 3, kzt.at[1], kzt_sem.at[1], at.at_zh(-1))
    send_k(2, 2, kx2.at[1], kx2_sem.at[1], at.at_x(2))
    for dz in (2, 1, 3, 0):
        send_k(1, dz, kx1.at[dz], kx1_sem.at[dz], at.at_x(1))
        send_k(3, dz, kx1.at[4 + dz], kx1_sem.at[4 + dz], at.at_x(-1))
    for dzl in (1, 0):
        for dy in (2, 1, 3, 0):
            slot = dy * 2 + dzl
            qcst[slot] = qp[qslot(dy, dzl, 1)].astype(BF16)
            out.go(qcst.at[slot], qcin.at[slot], qc_sem.at[slot], at.at_core())

    def core_sum(dy, dzl):
        slot = dy * 2 + dzl
        got(qcin.at[slot], qc_sem.at[slot])
        return qp[qslot(dy, dzl, 0)] + qcin[slot].astype(F32)

    for dzl in (1, 0):
        for dy in (2, 1, 3):
            slot = dy * 2 + dzl
            qst[slot] = core_sum(dy, dzl).astype(BF16)
            out.go(qst.at[slot], qyin.at[slot], qy_sem.at[slot], at.at_y(dy if dy < 3 else -1))
        qsum[dzl] = core_sum(0, dzl)

    for side in (0, 1):
        got(kzt.at[side], kzt_sem.at[side])
    kst[kslot(2, 0)] = (kp[kslot(2, 0)] + kzt[0].astype(F32) + kzt[1].astype(F32)).astype(BF16)
    out.go(kst.at[kslot(2, 0)], kx2.at[0], kx2_sem.at[0], at.at_x(2))

    def k_sum(dz):
        got(kx1.at[dz], kx1_sem.at[dz])
        got(kx1.at[4 + dz], kx1_sem.at[4 + dz])
        return kp[kslot(0, dz)] + kx1[dz].astype(F32) + kx1[4 + dz].astype(F32)

    total = k_sum(2)
    got(kx2.at[1], kx2_sem.at[1])
    kst[2] = (total + kx2[1].astype(F32)).astype(BF16)
    out.go(kst.at[2], kzin.at[2], kzin_sem.at[2], at.at_zh(2))
    for dz in (1, 3):
        kst[dz] = k_sum(dz).astype(BF16)
        out.go(kst.at[dz], kzin.at[dz], kzin_sem.at[dz], at.at_zh(dz if dz < 3 else -1))

    def y_sum(dzl):
        total = qsum[dzl]
        for dy in (1, 3, 2):
            slot = dy * 2 + dzl
            got(qyin.at[slot], qy_sem.at[slot])
            total = total + qyin[slot].astype(F32)
        return total

    qzst[...] = y_sum(1).astype(BF16)
    out.go(qzst, qzin, qz_sem.at[0], at.at_zl())
    qsum[0] = y_sum(0)

    total = k_sum(0)
    got(kx2.at[0], kx2_sem.at[0])
    total = total + kx2[0].astype(F32)
    got(qzin, qz_sem.at[0])
    q_out[...] = qsum[0] + qzin[...].astype(F32)
    for dz in (1, 3, 2):
        got(kzin.at[dz], kzin_sem.at[dz])
        total = total + kzin[dz].astype(F32)
    k_out[...] = total
    out.finish()


def reduce_scatter(q_terms, k_terms):
    _, rows, width = q_terms.shape
    vmem = pl.BlockSpec(memory_space=pltpu.VMEM)
    own = jax.ShapeDtypeStruct((rows, width), F32)

    def buf(*lead, dtype=BF16):
        return pltpu.VMEM((*lead, rows, width), dtype)

    def sems(count):
        return pltpu.SemaphoreType.DMA((count,))

    return pl.pallas_call(
        reduce_kernel,
        out_shape=(own, own),
        in_specs=[vmem, vmem],
        out_specs=(vmem, vmem),
        scratch_shapes=[
            buf(16), buf(8), buf(2), buf(2), buf(4),
            buf(8), buf(8), buf(2, dtype=F32), buf(8), buf(8), buf(), buf(),
            sems(32), sems(8), sems(2), sems(2), sems(4), sems(8), sems(8), sems(1),
        ],
        compiler_params=pltpu.CompilerParams(
            collective_id=1, has_side_effects=True, vmem_limit_bytes=48 * 2**20
        ),
        name="reduce_terms",
    )(q_terms, k_terms)


def local(queries, keys):
    frames = queries.shape[0] * lax.axis_size("row")
    _, rows, width = queries.shape
    whole_q, whole_k = gather(queries[0], keys[0])
    query_frame = whole_q.reshape(16 * rows, width)
    key_frame = whole_k.reshape(16 * rows, width)
    cols_half, grad_warp, score_half, residual = cycle_terms(
        query_frame, key_frame, width**-0.5, frames
    )
    q_term = jnp.dot(cols_half, grad_warp, preferred_element_type=jnp.float32)
    q_term = q_term + jnp.dot(score_half, key_frame, preferred_element_type=jnp.float32) - residual
    k_term = contract(score_half, query_frame, 0, 0)
    out_q, out_k = reduce_scatter(q_term.reshape(16, rows, width), k_term.reshape(16, rows, width))
    return (out_q[None], out_k[None])


def solution(mesh):
    placed = (P("row", "col", None), P("col", "row", None))
    return jax.shard_map(
        local,
        mesh=mesh,
        in_specs=placed,
        out_specs=(P("row", "col", None), P("col", "row", None)),
        check_vma=False,
    )
```

time: 82.2 us -> 75.3 us (0.916)
  the two profiles are of different devices: /device:TPU:8 before, /device:TPU:1 now
where the time goes in v2:
time: 75.3 us; the launch traced here: 75 us
  Pallas kernels  49.1 us (65%)
  matrix products  12.8 us (17%)
  local copies, waits for them, and re-layouts  7.53 us (10%)
  other arithmetic  4.81 us (6%)
  between operations  0.76 us (1%)
    pallas_call x1, Pallas kernels, gather(): pl.pallas_call(gather_kernel, out_shape=(full, full), in_specs=[vmem, vme...  23.8 us
    pallas_call x1, Pallas kernels, reduce_scatter(): pl.pallas_call(reduce_kernel, out_shape=(own, own), in_specs=[vmem, vmem]...  19.9 us
    dot_general x6, matrix products, contract(): lax.dot_general(left_side, right_side, (((left_dim,), (right_dim,)), ((),...  10.4 us
    unnamed x1, Pallas kernels  5.36 us
    unnamed x20, local copies, waits for them, and re-layouts  5.15 us
    convert_element_type x1, local copies, waits for them, and re-layouts, cycle_terms(): score_half = (score_scale * grad_scores).astype(jnp.bfloat16)  2.37 us
    convert_element_type x1, other arithmetic, cycle_terms(): resid_half = residual.astype(jnp.bfloat16)  2.1 us
    convert_element_type x1, other arithmetic, cycle_terms(): score_half = (score_scale * grad_scores).astype(jnp.bfloat16)  1.71 us

profile of v2, /device:TPU:1, one launch (start us, length us, event | category | flops | bytes accessed | tf_op | source)
XLA Modules:
  0.0 75.0 jit_solution(13730360122841363464)
XLA Ops:
  0.6 0.0 copy-start.2
  0.6 0.9 %copy-done.2 = bf16[1,48,768]{2,1,0:T(8,128)(2,1)S(1)} copy-done((bf16[1,48,768]{2,1,0:T(8,128)(2,1)S(1)}, bf16[1,48,768]{2,1,0:T(8,128)(2,1)}, u32[]{:S(2)}) %copy-start.2) | copy-done | bytes 73752
  1.5 0.0 copy-start.3
  1.5 0.9 %copy-done.3 = bf16[1,48,768]{2,1,0:T(8,128)(2,1)S(1)} copy-done((bf16[1,48,768]{2,1,0:T(8,128)(2,1)S(1)}, bf16[1,48,768]{2,1,0:T(8,128)(2,1)}, u32[]{:S(2)}) %copy-start.3) | copy-done | bytes 73752
  2.4 23.8 %gather_frames.1 = (bf16[16,48,768]{2,1,0:T(8,128)(2,1)S(1)}, bf16[16,48,768]{2,1,0:T(8,128)(2,1)S(1)}) custom-call(bf16[48,768]{1,0:T(8,128)(2,1)S(1)} %bitcast.34, bf16[48,768]{1,0:T(8,128)(2,1)S(1)} %bitcast.35), custom_call_target="tpu_custom_call" | custom-call | tf_op jit(solution)/shard_map/gather_frames/pallas_call | solution.py:185
  26.2 0.0 copy-start
  26.2 1.2 %fusion.15 = (f32[768]{0:T(1024)S(1)}, f32[768]{0:T(1024)S(1)}, f32[768,768]{1,0:T(8,128)S(1)}) fusion(bf16[768,768]{1,0:T(8,128)(2,1)S(1)} %bitcast.25, bf16[768,768]{1,0:T(8,128)(2,1)S(1)} %bitcast.30), kind=kOutput, calls=%fused_computation.21 | convolution fusion | flops 907737600 | bytes 4724736 | tf_op jit(solution)/shard_map/dot_general | solution.py:14
  27.4 0.0 copy-done
  27.4 0.0 copy-start.4
  27.4 1.0 %fusion.3 = (f32[768]{0:T(1024)S(1)}, f32[768]{0:T(1024)S(1)}) fusion(f32[768,768]{1,0:T(8,128)S(1)} %get-tuple-element.16, f32[768]{0:T(1024)S(1)} %get-tuple-element.14, f32[768]{0:T(1024)S(1)} %get-tuple-element.15), kind=kLoop, calls=%fused_computation.10 | loop fusion | flops 2357760 | bytes 2371584 | tf_op jit(solution)/shard_map/reduce_sum | solution.py:24
  28.4 2.6 %fusion.10 = f32[768,768]{1,0:T(8,128)} fusion(bf16[768,768]{1,0:T(8,128)(2,1)S(1)} %bitcast.26, f32[768,768]{1,0:T(8,128)S(1)} %get-tuple-element.16, f32[768]{0:T(1024)S(1)} %get-tuple-element.13, f32[768]{0:T(1024)S(1)} %get-tuple-element.15), kind=kOutput, calls=%fused_computation.19 | convolution fusion | flops 907739136 | bytes 5904384 | tf_op jit(solution)/shard_map/dot_general | solution.py:14
  31.0 0.0 copy-done.4
  31.0 5.4 %online-softmax = f32[768,768]{1,0:T(8,128)} custom-call(f32[768,768]{1,0:T(8,128)} %copy-done.4, f32[768,768]{1,0:T(8,128)} %fusion.10), custom_call_target="tpu_custom_call" | custom-call | tf_op online-softmax
  36.4 0.0 copy-start.5
  36.4 2.1 %fusion.4 = bf16[768,768]{1,0:T(8,128)(2,1)S(1)} fusion(f32[768,768]{1,0:T(8,128)} %online-softmax, bf16[16,48,768]{2,1,0:T(8,128)(2,1)S(1)} %get-tuple-element.6), kind=kLoop, calls=%fused_computation.13 | loop fusion | flops 2359296 | bytes 4718592 | tf_op jit(solution)/shard_map/convert_element_type | solution.py:31
  38.5 0.3 copy-done.5
  38.7 1.6 %convolution_convert_fusion = bf16[768,768]{1,0:T(8,128)(2,1)S(1)} fusion(bf16[768,768]{1,0:T(8,128)(2,1)S(1)} %fusion.4, f32[768,768]{1,0:T(8,128)S(1)} %copy-done.5, f32[768]{0:T(1024)S(1)} %get-tuple-element.12, f32[768]{0:T(1024)S(1)} %get-tuple-element.14), kind=kOutput, calls=%fused_computation.12 | convolution fusion | flops 908328960 | bytes 4724736 | tf_op jit(solution)/shard_map/dot_general | solution.py:14
  40.3 0.0 copy-start.8
  40.3 1.1 %fusion.16 = f32[768,768]{1,0:T(8,128)S(1)} fusion(bf16[768,768]{1,0:T(8,128)(2,1)S(1)} %bitcast.27, bf16[768,768]{1,0:T(8,128)(2,1)S(1)} %convolution_convert_fusion), kind=kOutput, calls=%fused_computation.22 | convolution fusion | flops 905969664 | bytes 4718592 | tf_op jit(solution)/shard_map/dot_general | solution.py:14
  41.4 0.5 copy-done.8
  42.0 1.6 %multiply_reduce_fusion.1 = (f32[768]{0:T(1024)S(1)}, f32[768]{0:T(1024)S(1)}, f32[768,768]{1,0:T(8,128)S(1)}) fusion(f32[768]{0:T(1024)S(1)} %get-tuple-element.12, f32[768,768]{1,0:T(8,128)S(1)} %copy-done.5, f32[768]{0:T(1024)S(1)} %get-tuple-element.14, f32[768,768]{1,0:T(8,128)S(1)} %fusion.16, f32[768]{0:T(1024)S(1)} %get-tuple-element.13, ...), kind=kOutput, calls=%fused_computation.3 | convolution fusion | flops 911276544 | bytes 10635264 | tf_op jit(solution)/shard_map/dot_general | solution.py:14
  43.6 1.7 %multiply_convert_fusion = bf16[768,768]{1,0:T(8,128)(2,1)S(1)} fusion(f32[768,768]{1,0:T(8,128)S(1)} %fusion.16, f32[768,768]{1,0:T(8,128)S(1)} %get-tuple-element.17, f32[768]{0:T(1024)S(1)} %get-tuple-element.11, f32[768]{0:T(1024)S(1)} %get-tuple-element.10, f32[768]{0:T(1024)S(1)} %get-tuple-element.13, f32[768,768]{1,0:T(8,128)S(1)} %copy-done.5, ...), kind=kLoop, calls=%fused_computation.1 | loop fusion | flops 6488064 | bytes 8275968 | tf_op jit(solution)/shard_map/convert_element_type | solution.py:39
  45.3 0.0 copy-start.7
  45.3 0.0 copy-start.1
  45.3 0.0 copy-start.6
  45.3 1.2 %fusion.8 = f32[768,768]{1,0:T(8,128)S(1)} fusion(bf16[768,768]{1,0:T(8,128)(2,1)S(1)} %convolution_convert_fusion, f32[768,768]{1,0:T(8,128)S(1)} %copy-done.5, f32[768]{0:T(1024)S(1)} %get-tuple-element.13, f32[768]{0:T(1024)S(1)} %get-tuple-element.15), kind=kOutput, calls=%fused_computation.17 | convolution fusion | flops 907739136 | bytes 5904384 | tf_op jit(solution)/shard_map/dot_general | solution.py:325
  46.5 0.0 copy-done.7
  46.5 0.5 copy-done.1
  47.0 0.7 copy-done.6
  47.7 1.3 %add_subtract_fusion = f32[768,768]{1,0:T(8,128)S(1)} fusion(f32[768,768]{1,0:T(8,128)S(1)} %fusion.8, bf16[768,768]{1,0:T(8,128)(2,1)S(1)} %multiply_convert_fusion, bf16[768,768]{1,0:T(8,128)(2,1)S(1)} %bitcast.31, f32[768,768]{1,0:T(8,128)S(1)} %copy-done.6, bf16[768,768]{1,0:T(8,128)(2,1)S(1)} %bitcast.28), kind=kOutput, calls=%fused_computation | convolution fusion | flops 908918784 | bytes 10616832 | tf_op jit(solution)/shard_map/dot_general | solution.py:326
  49.0 2.4 %copy.15 = bf16[768,768]{1,0:T(8,128)(2,1)} copy(bf16[768,768]{0,1:T(8,128)(2,1)} %bitcast.36) | data formatting | bytes 2359296 | tf_op jit(solution)/shard_map/convert_element_type | solution.py:39
  51.4 2.3 %fusion.17.kp = f32[16,48,768]{2,1,0:T(8,128)S(1)} fusion(bf16[16,48,768]{2,1,0:T(8,128)(2,1)} %bitcast.37, bf16[768,768,1]{1,0,2:T(8,128)(2,1)S(1)} %bitcast.29), kind=kOutput, calls=%fused_computation.23 | convolution fusion | flops 905969664 | bytes 4718592 | tf_op jit(solution)/shard_map/dot_general | solution.py:14
  53.7 19.9 %reduce_terms.1 = (f32[48,768]{1,0:T(8,128)S(1)}, f32[48,768]{1,0:T(8,128)S(1)}) custom-call(f32[16,48,768]{2,1,0:T(8,128)S(1)} %bitcast.24, f32[16,48,768]{2,1,0:T(8,128)S(1)} %fusion.17.kp), custom_call_target="tpu_custom_call" | custom-call | tf_op jit(solution)/shard_map/reduce_terms/pallas_call | solution.py:299
  73.7 0.7 copy.21
  74.4 0.7 copy.22
Async XLA Ops:
  0.6 0.9 %copy-start.2 = (bf16[1,48,768]{2,1,0:T(8,128)(2,1)S(1)}, bf16[1,48,768]{2,1,0:T(8,128)(2,1)}, u32[]{:S(2)}) copy-start(bf16[1,48,768]{2,1,0:T(8,128)(2,1)} %param.2) | copy-start | bytes 221188
  1.5 0.9 %copy-start.3 = (bf16[1,48,768]{2,1,0:T(8,128)(2,1)S(1)}, bf16[1,48,768]{2,1,0:T(8,128)(2,1)}, u32[]{:S(2)}) copy-start(bf16[1,48,768]{2,1,0:T(8,128)(2,1)} %param.3) | copy-start | bytes 221188
  26.2 1.2 %copy-start = (bf16[16,48,768]{2,1,0:T(8,128)(2,1)}, bf16[16,48,768]{2,1,0:T(8,128)(2,1)S(1)}, u32[]{:S(2)}) copy-start(bf16[16,48,768]{2,1,0:T(8,128)(2,1)S(1)} %get-tuple-element.7) | copy-start | bytes 3538948
  27.4 3.6 %copy-start.4 = (f32[768,768]{1,0:T(8,128)}, f32[768,768]{1,0:T(8,128)S(1)}, u32[]{:S(2)}) copy-start(f32[768,768]{1,0:T(8,128)S(1)} %get-tuple-element.16) | copy-start | bytes 7077892
  36.4 2.4 %copy-start.5 = (f32[768,768]{1,0:T(8,128)S(1)}, f32[768,768]{1,0:T(8,128)}, u32[]{:S(2)}) copy-start(f32[768,768]{1,0:T(8,128)} %copy-done.4) | copy-start | bytes 7077892
  40.3 1.7 %copy-start.8 = (f32[768,768]{1,0:T(8,128)S(1)}, f32[768,768]{1,0:T(8,128)}, u32[]{:S(2)}) copy-start(f32[768,768]{1,0:T(8,128)} %fusion.10) | copy-start | bytes 7077892
  45.3 1.2 %copy-start.7 = (bf16[768,768]{1,0:T(8,128)(2,1)}, bf16[768,768]{1,0:T(8,128)(2,1)S(1)}, u32[]{:S(2)}) copy-start(bf16[768,768]{1,0:T(8,128)(2,1)S(1)} %multiply_convert_fusion) | copy-start | bytes 3538948
  45.3 1.7 %copy-start.1 = (bf16[16,48,768]{2,1,0:T(8,128)(2,1)S(1)}, bf16[16,48,768]{2,1,0:T(8,128)(2,1)}, u32[]{:S(2)}) copy-start(bf16[16,48,768]{2,1,0:T(8,128)(2,1)} %copy-done) | copy-start | bytes 3538948
  45.3 2.4 %copy-start.6 = (f32[768,768]{1,0:T(8,128)S(1)}, f32[768,768]{1,0:T(8,128)}, u32[]{:S(2)}) copy-start(f32[768,768]{1,0:T(8,128)} %online-softmax) | copy-start | bytes 7077892

commit v3 on v2

--- a/solution.py
+++ b/solution.py
@@ -1,3 +1,6 @@
+import functools
+import math
+
 import jax
 import jax.numpy as jnp
 from jax import lax
@@ -8,36 +11,6 @@
 MESH = pl.DeviceIdType.MESH
 BF16 = jnp.bfloat16
 F32 = jnp.float32
-
-
-def contract(left_side, right_side, left_dim, right_dim):
-    return lax.dot_general(
-        left_side,
-        right_side,
-        (((left_dim,), (right_dim,)), ((), ())),
-        preferred_element_type=jnp.float32,
-    )
-
-
-def cycle_terms(query_frame, key_frame, score_scale, frames):
-    scores = score_scale * contract(query_frame, key_frame, 1, 1)
-    by_rows = jax.nn.softmax(scores, axis=1)
-    by_cols = jax.nn.softmax(scores, axis=0)
-    rows_half = by_rows.astype(jnp.bfloat16)
-    cols_half = by_cols.astype(jnp.bfloat16)
-    warped = contract(cols_half, query_frame, 0, 0).astype(jnp.bfloat16)
-    cycled = jnp.dot(rows_half, warped, preferred_element_type=jnp.float32)
-    residual = (cycled - query_frame.astype(jnp.float32)) / frames
-    resid_half = residual.astype(jnp.bfloat16)
-    grad_rows = contract(resid_half, warped, 1, 1)
-    grad_warp = contract(rows_half, resid_half, 0, 0).astype(jnp.bfloat16)
-    grad_cols = contract(query_frame, grad_warp, 1, 1)
-    grad_scores = by_rows * (grad_rows - jnp.sum(grad_rows * by_rows, axis=1, keepdims=True))
-    grad_scores = grad_scores + by_cols * (
-        grad_cols - jnp.sum(grad_cols * by_cols, axis=0, keepdims=True)
-    )
-    score_half = (score_scale * grad_scores).astype(jnp.bfloat16)
-    return (cols_half, grad_warp, score_half, residual)
 
 
 class Place:
@@ -313,18 +286,141 @@
     )(q_terms, k_terms)
 
 
+TOK = 768
+KC = 192
+
+
+def nt(a, b):
+    return lax.dot_general(a, b, (((1,), (1,)), ((), ())), preferred_element_type=F32)
+
+
+def nn(a, b):
+    return lax.dot_general(a, b, (((1,), (0,)), ((), ())), preferred_element_type=F32)
+
+
+def tn(a, b):
+    return lax.dot_general(a, b, (((0,), (0,)), ((), ())), preferred_element_type=F32)
+
+
+def fold(x, op):
+    return op(x.reshape(x.shape[0] // 8, 8, x.shape[1]), axis=0)
+
+
+class Pair:
+    def __init__(self, scale, frames, qf, kf, st, bt, at, bh, ah, v, gr, gh, da, dv, ds, cmax, csum, cdel):
+        self.__dict__.update(locals())
+
+    def scores(self, c):
+        rows = pl.ds(c * KC, KC)
+        st = nt(self.kf[rows], self.qf[...]) * (self.scale * math.log2(math.e))
+        self.st[rows] = st
+        top = fold(st, jnp.max)
+        self.cmax[...] = top if c == 0 else jnp.maximum(self.cmax[...], top)
+        e = jnp.exp2(st - jnp.max(st, axis=1, keepdims=True))
+        b = e * (1.0 / jnp.sum(e, axis=1, keepdims=True))
+        self.bt[rows] = b
+        bh = b.astype(BF16)
+        self.bh[rows] = bh
+        self.v[rows] = nn(bh, self.qf[...]).astype(BF16)
+
+    def attend(self):
+        top = jnp.max(self.cmax[...], axis=0, keepdims=True)
+        total = jnp.zeros((8, TOK), F32)
+        for c in range(TOK // KC):
+            rows = pl.ds(c * KC, KC)
+            e = jnp.exp2(self.st[rows] - top)
+            self.at[rows] = e
+            total = total + fold(e, jnp.sum)
+        inv = 1.0 / jnp.sum(total, axis=0, keepdims=True)
+        for c in range(TOK // KC):
+            rows = pl.ds(c * KC, KC)
+            a = self.at[rows] * inv
+            self.at[rows] = a
+            self.ah[rows] = a.astype(BF16)
+
+    def residual(self, size=384):
+        for c in range(TOK // size):
+            rows = pl.ds(c * size, size)
+            cycled = tn(self.ah[:, rows], self.v[...])
+            g = (cycled - self.qf[rows].astype(F32)) * (1.0 / self.frames)
+            self.gr[rows] = g
+            self.gh[rows] = g.astype(BF16)
+
+    def grad_rows(self, size=384):
+        total = jnp.zeros((8, TOK), F32)
+        for c in range(TOK // size):
+            rows = pl.ds(c * size, size)
+            da = nt(self.v[rows], self.gh[...])
+            self.da[rows] = da
+            total = total + fold(da * self.at[rows], jnp.sum)
+        self.cdel[...] = jnp.broadcast_to(jnp.sum(total, axis=0, keepdims=True), (8, TOK))
+
+    def grad_warp(self, size=384):
+        for c in range(TOK // size):
+            rows = pl.ds(c * size, size)
+            self.dv[rows] = nn(self.ah[rows], self.gh[...]).astype(BF16)
+
+    def grad_scores(self, c, size=KC):
+        rows = pl.ds(c * size, size)
+        db = nt(self.dv[rows], self.qf[...])
+        b = self.bt[rows]
+        delta = jnp.sum(db * b, axis=1, keepdims=True)
+        ds = self.at[rows] * (self.da[rows] - self.cdel[0:1]) + b * (db - delta)
+        dsh = (ds * self.scale).astype(BF16)
+        self.ds[rows] = dsh
+        return nn(dsh, self.qf[...])
+
+    def query_terms(self, c, size=384):
+        rows = pl.ds(c * size, size)
+        return tn(self.bh[:, rows], self.dv[...]) + tn(self.ds[:, rows], self.kf[...]) - self.gr[rows]
+
+
+def pair_scratch():
+    def whole(dtype):
+        return pltpu.VMEM((TOK, TOK), dtype)
+
+    return [
+        whole(F32), whole(F32), whole(F32), whole(BF16), whole(BF16), whole(BF16),
+        whole(F32), whole(BF16), whole(F32), whole(BF16), whole(BF16),
+        pltpu.VMEM((8, TOK), F32), pltpu.VMEM((8, TOK), F32), pltpu.VMEM((8, TOK), F32),
+    ]
+
+
+def pair_kernel(scale, frames, qf, kf, q_out, k_out, *scratch):
+    pair = Pair(scale, frames, qf, kf, *scratch)
+    for c in range(TOK // KC):
+        pair.scores(c)
+    pair.attend()
+    pair.residual()
+    pair.grad_rows()
+    pair.grad_warp()
+    for c in range(TOK // KC):
+        k_out[pl.ds(c * KC, KC)] = pair.grad_scores(c)
+    for c in range(2):
+        q_out[pl.ds(c * 384, 384)] = pair.query_terms(c)
+
+
+def pair_terms(whole_q, whole_k, scale, frames):
+    vmem = pl.BlockSpec(memory_space=pltpu.VMEM)
+    full = jax.ShapeDtypeStruct((TOK, TOK), F32)
+    return pl.pallas_call(
+        functools.partial(pair_kernel, scale, frames),
+        out_shape=(full, full),
+        in_specs=[vmem, vmem],
+        out_specs=(vmem, vmem),
+        scratch_shapes=pair_scratch(),
+        compiler_params=pltpu.CompilerParams(vmem_limit_bytes=48 * 2**20),
+        name="pair_terms",
+    )(whole_q, whole_k)
+
+
 def local(queries, keys):
     frames = queries.shape[0] * lax.axis_size("row")
     _, rows, width = queries.shape
     whole_q, whole_k = gather(queries[0], keys[0])
-    query_frame = whole_q.reshape(16 * rows, width)
-    key_frame = whole_k.reshape(16 * rows, width)
-    cols_half, grad_warp, score_half, residual = cycle_terms(
-        query_frame, key_frame, width**-0.5, frames
+    q_term, k_term = pair_terms(
+        whole_q.reshape(16 * rows, width), whole_k.reshape(16 * rows, width), width**-0.5, frames
     )
-    q_term = jnp.dot(cols_half, grad_warp, preferred_element_type=jnp.float32)
-    q_term = q_term + jnp.dot(score_half, key_frame, preferred_element_type=jnp.float32) - residual
-    k_term = contract(score_half, query_frame, 0, 0)
     out_q, out_k = reduce_scatter(q_term.reshape(16, rows, width), k_term.reshape(16, rows, width))
     return (out_q[None], out_k[None])
 

time: 75.3 us -> 62.2 us (0.83)
  matrix products: 12.8 us -> 0 us
  Pallas kernels: 49.1 us -> 56.6 us
  other arithmetic: 4.81 us -> 0 us
  local copies, waits for them, and re-layouts: 7.53 us -> 4.74 us
    pallas_call x0 -> x1, Pallas kernels: none -> 13.2 us  [pair_terms(): pl.pallas_call(functools.partial(pair_kernel, scale, frames), out_shape=(...]
    dot_general x8 -> x0, matrix products: 12.8 us -> none  [the longest x6 10.4 us: contract(): lax.dot_general(left_side, right_side, (((left_dim,), (right_dim,)), ((),...]
    unnamed x1 -> x0, Pallas kernels: 5.36 us -> none
    convert_element_type x2 -> x0, other arithmetic: 3.8 us -> none  [the longest x1 2.1 us: cycle_terms(): resid_half = residual.astype(jnp.bfloat16)]
    convert_element_type x1 -> x0, local copies, waits for them, and re-layouts: 2.37 us -> none  [cycle_terms(): score_half = (score_scale * grad_scores).astype(jnp.bfloat16)]
    reduce_sum x1 -> x0, other arithmetic: 1.01 us -> none  [cycle_terms(): by_rows = jax.nn.softmax(scores, axis=1)]
    unnamed x20 -> x8, local copies, waits for them, and re-layouts: 5.15 us -> 4.74 us
where the time goes in v3:
time: 62.2 us; the launch traced here: 62 us
  Pallas kernels  56.6 us (91%)
  local copies, waits for them, and re-layouts  4.74 us (8%)
  between operations  0.67 us (1%)
    pallas_call x1, Pallas kernels, gather(): pl.pallas_call(gather_kernel, out_shape=(full, full), in_specs=[vmem, vme...  23.8 us
    pallas_call x1, Pallas kernels, reduce_scatter(): pl.pallas_call(reduce_kernel, out_shape=(own, own), in_specs=[vmem, vmem]...  19.7 us
    pallas_call x1, Pallas kernels, pair_terms(): pl.pallas_call(functools.partial(pair_kernel, scale, frames), out_shape=(...  13.2 us
    unnamed x8, local copies, waits for them, and re-layouts  4.74 us

profile of v3, /device:TPU:1, one launch (start us, length us, event | category | flops | bytes accessed | tf_op | source)
XLA Modules:
  0.0 62.0 jit_solution(17103894784633343346)
XLA Ops:
  0.6 0.0 copy-start.1
  0.6 0.9 %copy-done.1 = bf16[1,48,768]{2,1,0:T(8,128)(2,1)S(1)} copy-done((bf16[1,48,768]{2,1,0:T(8,128)(2,1)S(1)}, bf16[1,48,768]{2,1,0:T(8,128)(2,1)}, u32[]{:S(2)}) %copy-start.1) | copy-done | bytes 73752
  1.5 0.0 copy-start.2
  1.5 0.9 %copy-done.2 = bf16[1,48,768]{2,1,0:T(8,128)(2,1)S(1)} copy-done((bf16[1,48,768]{2,1,0:T(8,128)(2,1)S(1)}, bf16[1,48,768]{2,1,0:T(8,128)(2,1)}, u32[]{:S(2)}) %copy-start.2) | copy-done | bytes 73752
  2.4 23.8 %gather_frames.1 = (bf16[16,48,768]{2,1,0:T(8,128)(2,1)S(1)}, bf16[16,48,768]{2,1,0:T(8,128)(2,1)S(1)}) custom-call(bf16[48,768]{1,0:T(8,128)(2,1)S(1)} %bitcast.14, bf16[48,768]{1,0:T(8,128)(2,1)S(1)} %bitcast.15), custom_call_target="tpu_custom_call" | custom-call | tf_op jit(solution)/shard_map/gather_frames/pallas_call | solution.py:158
  26.2 13.2 %pair_terms.1 = (f32[768,768]{1,0:T(8,128)S(1)}, f32[768,768]{1,0:T(8,128)}) custom-call(bf16[768,768]{1,0:T(8,128)(2,1)S(1)} %bitcast.10, bf16[768,768]{1,0:T(8,128)(2,1)S(1)} %bitcast.11), custom_call_target="tpu_custom_call" | custom-call | tf_op jit(solution)/shard_map/pair_terms/pallas_call | solution.py:406
  39.3 0.0 copy-start
  39.3 1.7 %copy-done = f32[768,768]{1,0:T(8,128)S(1)} copy-done((f32[768,768]{1,0:T(8,128)S(1)}, f32[768,768]{1,0:T(8,128)}, u32[]{:S(2)}) %copy-start) | copy-done | bytes 2359320
  41.0 19.7 %reduce_terms.1 = (f32[48,768]{1,0:T(8,128)S(1)}, f32[48,768]{1,0:T(8,128)S(1)}) custom-call(f32[16,48,768]{2,1,0:T(8,128)S(1)} %bitcast.8, f32[16,48,768]{2,1,0:T(8,128)S(1)} %bitcast.9), custom_call_target="tpu_custom_call" | custom-call | tf_op jit(solution)/shard_map/reduce_terms/pallas_call | solution.py:272
  60.7 0.7 %copy.6 = f32[1,48,768]{2,1,0:T(8,128)} copy(f32[1,48,768]{2,1,0:T(8,128)S(1)} %bitcast.13) | data formatting | bytes 294912
  61.4 0.7 %copy.7 = f32[1,48,768]{2,1,0:T(8,128)} copy(f32[1,48,768]{2,1,0:T(8,128)S(1)} %bitcast.12) | data formatting | bytes 294912
Async XLA Ops:
  0.6 0.9 %copy-start.1 = (bf16[1,48,768]{2,1,0:T(8,128)(2,1)S(1)}, bf16[1,48,768]{2,1,0:T(8,128)(2,1)}, u32[]{:S(2)}) copy-start(bf16[1,48,768]{2,1,0:T(8,128)(2,1)} %param.2) | copy-start | bytes 221188
  1.5 0.9 %copy-start.2 = (bf16[1,48,768]{2,1,0:T(8,128)(2,1)S(1)}, bf16[1,48,768]{2,1,0:T(8,128)(2,1)}, u32[]{:S(2)}) copy-start(bf16[1,48,768]{2,1,0:T(8,128)(2,1)} %param.3) | copy-start | bytes 221188
  39.3 1.7 %copy-start = (f32[768,768]{1,0:T(8,128)S(1)}, f32[768,768]{1,0:T(8,128)}, u32[]{:S(2)}) copy-start(f32[768,768]{1,0:T(8,128)} %get-tuple-element.11) | copy-start | bytes 7077892

commit v4 on v0

v4 whole, which is shorter than its diff:
```python
import functools
import math

import jax
import jax.numpy as jnp
from jax import lax
from jax.experimental import pallas as pl
from jax.experimental.pallas import tpu as pltpu
from jax.sharding import PartitionSpec as P

MESH = pl.DeviceIdType.MESH
BF16 = jnp.bfloat16
F32 = jnp.float32


class Place:
    def __init__(self):
        row = lax.axis_index("row")
        col = lax.axis_index("col")
        self.zh, self.x = row // 4, row % 4
        self.y, self.zl, self.c = col // 4, (col // 2) % 2, col % 2
        self.row, self.col = row, col

    def at_x(self, step):
        return (self.zh * 4 + (self.x + step + 4) % 4, self.col)

    def at_zh(self, step):
        return (((self.zh + step + 4) % 4) * 4 + self.x, self.col)

    def at_y(self, step):
        return (self.row, ((self.y + step + 4) % 4) * 4 + self.zl * 2 + self.c)

    def at_zl(self):
        return (self.row, self.y * 4 + (1 - self.zl) * 2 + self.c)

    def at_core(self):
        return (self.row, self.y * 4 + self.zl * 2 + 1 - self.c)


def greet(at):
    barrier = pltpu.get_barrier_semaphore()
    others = [at.at_core(), at.at_zl()]
    for step in (1, -1, 2):
        others += [at.at_x(step), at.at_y(step), at.at_zh(step)]
    for other in others:
        pl.semaphore_signal(barrier, inc=1, device_id=other, device_id_type=MESH)
    pl.semaphore_wait(barrier, len(others))


class Sends:
    def __init__(self, send_sem):
        self.send_sem = send_sem
        self.started = []

    def go(self, src, dst, recv, device):
        copy = pltpu.make_async_remote_copy(
            src_ref=src,
            dst_ref=dst,
            send_sem=self.send_sem.at[len(self.started)],
            recv_sem=recv,
            device_id=device,
            device_id_type=MESH,
        )
        copy.start()
        self.started.append(copy)

    def finish(self):
        for copy in self.started:
            copy.wait_send()


TOK = 768
ROWS = 48
KC = 192


def nt(a, b):
    return lax.dot_general(a, b, (((1,), (1,)), ((), ())), preferred_element_type=F32)


def nn(a, b):
    return lax.dot_general(a, b, (((1,), (0,)), ((), ())), preferred_element_type=F32)


def tn(a, b):
    return lax.dot_general(a, b, (((0,), (0,)), ((), ())), preferred_element_type=F32)


def fold(x, op):
    return op(x.reshape(x.shape[0] // 8, 8, x.shape[1]), axis=0)


class Pair:
    def __init__(self, scale, frames, qf, kf, st, bt, at, bh, ah, v, gr, gh, da, dv, ds, cmax, csum, cdel):
        self.__dict__.update(locals())

    def scores(self, c):
        rows = pl.ds(c * KC, KC)
        st = nt(self.kf[rows], self.qf[...]) * (self.scale * math.log2(math.e))
        self.st[rows] = st
        top = fold(st, jnp.max)
        self.cmax[...] = top if c == 0 else jnp.maximum(self.cmax[...], top)
        e = jnp.exp2(st - jnp.max(st, axis=1, keepdims=True))
        b = e * (1.0 / jnp.sum(e, axis=1, keepdims=True))
        self.bt[rows] = b
        bh = b.astype(BF16)
        self.bh[rows] = bh
        self.v[rows] = nn(bh, self.qf[...]).astype(BF16)

    def attend(self):
        top = jnp.max(self.cmax[...], axis=0, keepdims=True)
        total = jnp.zeros((8, TOK), F32)
        for c in range(TOK // KC):
            rows = pl.ds(c * KC, KC)
            e = jnp.exp2(self.st[rows] - top)
            self.at[rows] = e
            total = total + fold(e, jnp.sum)
        inv = 1.0 / jnp.sum(total, axis=0, keepdims=True)
        for c in range(TOK // KC):
            rows = pl.ds(c * KC, KC)
            a = self.at[rows] * inv
            self.at[rows] = a
            self.ah[rows] = a.astype(BF16)

    def residual(self, size=384):
        for c in range(TOK // size):
            rows = pl.ds(c * size, size)
            cycled = tn(self.ah[:, rows], self.v[...])
            g = (cycled - self.qf[rows].astype(F32)) * (1.0 / self.frames)
            self.gr[rows] = g
            self.gh[rows] = g.astype(BF16)

    def grad_rows(self, size=384):
        total = jnp.zeros((8, TOK), F32)
        for c in range(TOK // size):
            rows = pl.ds(c * size, size)
            da = nt(self.v[rows], self.gh[...])
            self.da[rows] = da
            total = total + fold(da * self.at[rows], jnp.sum)
        self.cdel[...] = jnp.broadcast_to(jnp.sum(total, axis=0, keepdims=True), (8, TOK))

    def grad_warp(self, size=384):
        for c in range(TOK // size):
            rows = pl.ds(c * size, size)
            self.dv[rows] = nn(self.ah[rows], self.gh[...]).astype(BF16)

    def grad_scores(self, c, size=KC):
        rows = pl.ds(c * size, size)
        db = nt(self.dv[rows], self.qf[...])
        b = self.bt[rows]
        delta = jnp.sum(db * b, axis=1, keepdims=True)
        ds = self.at[rows] * (self.da[rows] - self.cdel[0:1]) + b * (db - delta)
        dsh = (ds * self.scale).astype(BF16)
        self.ds[rows] = dsh
        return nn(dsh, self.qf[...])

    def query_terms(self, c, size=384):
        rows = pl.ds(c * size, size)
        return tn(self.bh[:, rows], self.dv[...]) + tn(self.ds[:, rows], self.kf[...]) - self.gr[rows]


def pair_scratch():
    def whole(dtype):
        return pltpu.VMEM((TOK, TOK), dtype)

    return [
        whole(F32), whole(F32), whole(F32), whole(BF16), whole(BF16), whole(BF16),
        whole(F32), whole(BF16), whole(F32), whole(BF16), whole(BF16),
        pltpu.VMEM((8, TOK), F32), pltpu.VMEM((8, TOK), F32), pltpu.VMEM((8, TOK), F32),
    ]


ZORDER = (0, 1, 3, 2)


def krow(dx, dz):
    return (ZORDER.index(dz % 4) * 4 + dx % 4) * ROWS


def qrow(dy, dzl, dc):
    return (((1 - dzl) * 2 + 1 - dc) * 4 + dy % 4) * ROWS


def cycle_kernel(scale, frames, q_hbm, k_hbm, q_out, k_out, qf, kf, *scratch):
    pair = Pair(scale, frames, qf, kf, *scratch[:14])
    (
        kst, kp, kx1, kx2, kzt, kzin, qcst, qcin, qp, qst, qyin, qzst, qzin,
        own_sem, send_sem, q_sem, k_sem,
        kx1_sem, kx2_sem, kzt_sem, kzin_sem, qc_sem, qy_sem, qz_sem,
    ) = scratch[14:]
    at = Place()

    def kblock(dx, dz):
        return kf.at[pl.ds(krow(dx, dz), ROWS)]

    def qblock(dy, dzl, dc):
        return qf.at[pl.ds(qrow(dy, dzl, dc), ROWS)]

    own_q = pltpu.make_async_copy(q_hbm.at[0], qblock(0, 0, 0), own_sem.at[0])
    own_k = pltpu.make_async_copy(k_hbm.at[0], kblock(0, 0), own_sem.at[1])
    own_q.start()
    own_k.start()
    greet(at)
    own_q.wait()
    own_k.wait()
    out = Sends(send_sem)

    def got(ref, sem):
        pltpu.make_async_remote_copy(
            src_ref=ref, dst_ref=ref, send_sem=send_sem.at[0],
            recv_sem=sem, device_id=at.at_core(), device_id_type=MESH,
        ).wait_recv()


    def ksem(dx, dz):
        return k_sem.at[krow(dx, dz) // ROWS]

    def qsem(dy, dzl, dc):
        return q_sem.at[qrow(dy, dzl, dc) // ROWS]

    def got_k(dx, dz):
        got(kblock(dx, dz), ksem(dx, dz))

    def got_q(dy, dzl, dc):
        got(qblock(dy, dzl, dc), qsem(dy, dzl, dc))

    def k_along_x(dz, steps):
        for step in steps:
            out.go(kblock(0, dz), kblock(-step, dz), ksem(-step, dz), at.at_x(step))

    def k_along_z(dx, steps):
        for step in steps:
            out.go(kblock(dx, 0), kblock(dx, -step), ksem(dx, -step), at.at_zh(step))

    def q_along_y(dzl):
        for step in (1, -1, 2):
            out.go(qblock(0, dzl, 0), qblock(-step, dzl, 0), qsem(-step, dzl, 0), at.at_y(step))

    def q_to_core(dy, dzl):
        out.go(qblock(dy, dzl, 0), qblock(dy, dzl, 1), qsem(dy, dzl, 1), at.at_core())

    out.go(qblock(0, 0, 0), qblock(0, 1, 0), qsem(0, 1, 0), at.at_zl())
    k_along_z(0, (1, -1))
    k_along_x(0, (1, -1))
    q_along_y(0)
    k_along_z(0, (2,))
    k_along_x(0, (2,))
    q_to_core(0, 0)

    got_q(0, 1, 0)
    q_along_y(1)
    q_to_core(0, 1)
    for dz in (1, 3):
        got_k(0, dz)
        k_along_x(dz, (1, -1))
    for dy in (1, 3, 2):
        got_q(dy, 0, 0)
        q_to_core(dy, 0)
    got_k(2, 0)
    k_along_z(2, (1, -1))
    got_k(0, 2)
    k_along_x(2, (1, -1, 2))
    for dy in (1, 3, 2):
        got_q(dy, 1, 0)
        q_to_core(dy, 1)
    for dzl in (0, 1):
        for dy in (0, 1, 3, 2):
            got_q(dy, dzl, 1)

    got_k(1, 0)
    got_k(3, 0)
    for c, dz in enumerate(ZORDER):
        if dz != 0:
            for dx in (1, 3, 2):
                got_k(dx, dz)
        pair.scores(c)
    pair.attend()
    pair.residual()
    pair.grad_rows()
    pair.grad_warp()

    def send_k(dx, dz, dst, sem, device):
        out.go(kst.at[pl.ds(krow(dx, dz), ROWS)], dst, sem, device)

    for c in (3, 1, 2, 0):
        dz = ZORDER[c]
        terms = pair.grad_scores(c)
        kst[pl.ds(c * KC, KC)] = terms.astype(BF16)
        kp[dz] = terms[0:ROWS]
        if dz == 0:
            kp[4] = terms[2 * ROWS : 3 * ROWS]
        if dz == 1:
            send_k(2, 1, kzt.at[0], kzt_sem.at[0], at.at_zh(1))
        if dz == 3:
            send_k(2, 3, kzt.at[1], kzt_sem.at[1], at.at_zh(-1))
        if dz == 2:
            send_k(2, 2, kx2.at[1], kx2_sem.at[1], at.at_x(2))
        send_k(1, dz, kx1.at[dz], kx1_sem.at[dz], at.at_x(1))
        send_k(3, dz, kx1.at[4 + dz], kx1_sem.at[4 + dz], at.at_x(-1))

    for dzl in (1, 0):
        terms = pair.query_terms(1 - dzl)
        rows = pl.ds(dzl * KC, KC)
        qcst[rows] = terms[0:KC].astype(BF16)
        qp[rows] = terms[KC : 2 * KC]
        for dy in (2, 1, 3, 0):
            slot = dzl * 4 + dy
            block = pl.ds(slot * ROWS, ROWS)
            out.go(qcst.at[block], qcin.at[block], qc_sem.at[slot], at.at_core())

    def core_sum(dy, dzl):
        slot = dzl * 4 + dy
        block = pl.ds(slot * ROWS, ROWS)
        got(qcin.at[block], qc_sem.at[slot])
        return qp[block] + qcin[block].astype(F32)

    def q_along_y_sums(dzl):
        for dy in (2, 1, 3):
            slot = dzl * 4 + dy
            qst[slot] = core_sum(dy, dzl).astype(BF16)
            out.go(qst.at[slot], qyin.at[slot], qy_sem.at[slot], at.at_y(dy if dy < 3 else -1))

    q_along_y_sums(1)
    q_along_y_sums(0)

    def k_sum(dz):
        got(kx1.at[dz], kx1_sem.at[dz])
        got(kx1.at[4 + dz], kx1_sem.at[4 + dz])
        return kp[dz] + kx1[dz].astype(F32) + kx1[4 + dz].astype(F32)

    def k_send_z(dz, total):
        kst[pl.ds(krow(0, dz), ROWS)] = total.astype(BF16)
        send_k(0, dz, kzin.at[dz], kzin_sem.at[dz], at.at_zh(dz if dz < 3 else -1))

    total = k_sum(2)
    got(kx2.at[1], kx2_sem.at[1])
    k_send_z(2, total + kx2[1].astype(F32))
    for side in (0, 1):
        got(kzt.at[side], kzt_sem.at[side])
    kst[pl.ds(krow(2, 0), ROWS)] = (kp[4] + kzt[0].astype(F32) + kzt[1].astype(F32)).astype(BF16)
    send_k(2, 0, kx2.at[0], kx2_sem.at[0], at.at_x(2))
    for dz in (1, 3):
        k_send_z(dz, k_sum(dz))

    def y_sum(dzl):
        total = core_sum(0, dzl)
        for dy in (1, 3, 2):
            slot = dzl * 4 + dy
            got(qyin.at[slot], qy_sem.at[slot])
            total = total + qyin[slot].astype(F32)
        return total

    qzst[...] = y_sum(1).astype(BF16)
    out.go(qzst, qzin, qz_sem.at[0], at.at_zl())
    q_total = y_sum(0)
    total = k_sum(0)
    got(kx2.at[0], kx2_sem.at[0])
    total = total + kx2[0].astype(F32)
    got(qzin, qz_sem.at[0])
    q_out[0] = q_total + qzin[...].astype(F32)
    for dz in (1, 3, 2):
        got(kzin.at[dz], kzin_sem.at[dz])
        total = total + kzin[dz].astype(F32)
    k_out[0] = total
    out.finish()


def local(queries, keys):
    frames = queries.shape[0] * lax.axis_size("row")
    scale = queries.shape[2] ** -0.5
    vmem = pl.BlockSpec(memory_space=pltpu.VMEM)
    hbm = pl.BlockSpec(memory_space=pltpu.MemorySpace.HBM)
    own = jax.ShapeDtypeStruct((1, ROWS, TOK), F32)

    def buf(*lead, dtype=BF16):
        return pltpu.VMEM((*lead, TOK), dtype)

    def sems(count):
        return pltpu.SemaphoreType.DMA((count,))

    return pl.pallas_call(
        functools.partial(cycle_kernel, scale, frames),
        out_shape=(own, own),
        in_specs=[hbm, hbm],
        out_specs=(vmem, vmem),
        scratch_shapes=[
            buf(TOK), buf(TOK),
            *pair_scratch(),
            buf(TOK), buf(5, ROWS, dtype=F32), buf(8, ROWS), buf(2, ROWS), buf(2, ROWS), buf(4, ROWS),
            buf(8 * ROWS), buf(8 * ROWS), buf(8 * ROWS, dtype=F32), buf(8, ROWS), buf(8, ROWS), buf(ROWS), buf(ROWS),
            sems(2), sems(60), sems(16), sems(16),
            sems(8), sems(2), sems(2), sems(4), sems(8), sems(8), sems(1),
        ],
        compiler_params=pltpu.CompilerParams(
            collective_id=0, has_side_effects=True, vmem_limit_bytes=60 * 2**20
        ),
        name="cycle_pairs",
    )(queries, keys)


def solution(mesh):
    placed = (P("row", "col", None), P("col", "row", None))
    return jax.shard_map(
        local,
        mesh=mesh,
        in_specs=placed,
        out_specs=(P("row", "col", None), P("col", "row", None)),
        check_vma=False,
    )
```

time: 294 us -> 53.9 us (0.18)
  waiting for transfers between devices: 245 us -> 0 us
  Pallas kernels: 5.36 us -> 50.9 us
  matrix products: 19.9 us -> 0 us
  between operations: 13.9 us -> 0.65 us
    reduce_scatter x2 -> x0, waiting for transfers between devices: 149 us -> none  [the longest x1 82 us: local(): out_k = lax.psum_scatter(grad_k, 'row', scatter_dimension=1, tiled=True)]
    all_gather x2 -> x0, waiting for transfers between devices: 94.5 us -> none  [the longest x1 54.2 us: local(): whole_k = lax.all_gather(keys, 'row', axis=1, tiled=True)]
    pallas_call x0 -> x1, Pallas kernels: none -> 50.9 us  [local(): pl.pallas_call(functools.partial(cycle_kernel, scale, frames), out_shape=...]
    dot_general x8 -> x0, matrix products: 19.9 us -> none  [the longest x6 14.7 us: contract(): lax.dot_general(left_side, right_side, (((left_dim,), (right_dim,)), ((),...]
    unnamed x1 -> x0, Pallas kernels: 5.36 us -> none
  transfers between devices with their start and end apart: 4 -> 0, of which waited for: 4 -> 0; matrix products, arithmetic and copies ran while one was open for 2% -> 0% of each run, Pallas kernels for 0% -> 0%
where the time goes in v4:
time: 53.9 us; the launch traced here: 53.8 us
  Pallas kernels  50.9 us (94%)
  local copies, waits for them, and re-layouts  2.28 us (4%)
  between operations  0.65 us (1%)
    pallas_call x1, Pallas kernels, local(): pl.pallas_call(functools.partial(cycle_kernel, scale, frames), out_shape=...  50.9 us
    unnamed x4, local copies, waits for them, and re-layouts  2.28 us

profile of v4, /device:TPU:1, one launch (start us, length us, event | category | flops | bytes accessed | tf_op | source)
XLA Modules:
  0.0 53.8 jit_solution(6038102807645773461)
XLA Ops:
  0.6 50.9 %cycle_pairs.1 = (f32[1,48,768]{2,1,0:T(8,128)}, f32[1,48,768]{2,1,0:T(8,128)}) custom-call(bf16[1,48,768]{2,1,0:T(8,128)(2,1)} %q_hbm.1, bf16[1,48,768]{2,1,0:T(8,128)(2,1)} %k_hbm.1), custom_call_target="tpu_custom_call" | custom-call | tf_op jit(solution)/shard_map/cycle_pairs/pallas_call | solution.py:381
  51.5 0.0 copy-start
  51.5 1.6 %copy.6 = f32[1,48,768]{2,1,0:T(8,128)} copy(f32[1,48,768]{2,1,0:T(8,128)} %get-tuple-element.4) | data formatting | bytes 294912
  53.1 0.0 copy-done
  53.1 0.7 %copy.7 = f32[1,48,768]{2,1,0:T(8,128)} copy(f32[1,48,768]{2,1,0:T(8,128)S(1)} %copy-done) | data formatting | bytes 294912
Async XLA Ops:
  51.5 1.6 %copy-start = (f32[1,48,768]{2,1,0:T(8,128)S(1)}, f32[1,48,768]{2,1,0:T(8,128)}, u32[]{:S(2)}) copy-start(f32[1,48,768]{2,1,0:T(8,128)} %get-tuple-element.5) | copy-start | bytes 442372

commit v5 on v4

--- a/solution.py
+++ b/solution.py
@@ -144,15 +144,16 @@
             rows = pl.ds(c * size, size)
             self.dv[rows] = nn(self.ah[rows], self.gh[...]).astype(BF16)
 
-    def grad_scores(self, c, size=KC):
+    def grad_scores(self, c, size=384):
         rows = pl.ds(c * size, size)
         db = nt(self.dv[rows], self.qf[...])
         b = self.bt[rows]
         delta = jnp.sum(db * b, axis=1, keepdims=True)
         ds = self.at[rows] * (self.da[rows] - self.cdel[0:1]) + b * (db - delta)
-        dsh = (ds * self.scale).astype(BF16)
-        self.ds[rows] = dsh
-        return nn(dsh, self.qf[...])
+        self.ds[rows] = (ds * self.scale).astype(BF16)
+
+    def key_terms(self, c, size=KC):
+        return nn(self.ds[pl.ds(c * size, size)], self.qf[...])
 
     def query_terms(self, c, size=384):
         rows = pl.ds(c * size, size)
@@ -241,10 +242,9 @@
 
     out.go(qblock(0, 0, 0), qblock(0, 1, 0), qsem(0, 1, 0), at.at_zl())
     k_along_z(0, (1, -1))
-    k_along_x(0, (1, -1))
+    k_along_x(0, (2, 1, -1))
     q_along_y(0)
     k_along_z(0, (2,))
-    k_along_x(0, (2,))
     q_to_core(0, 0)
 
     got_q(0, 1, 0)
@@ -259,7 +259,7 @@
     got_k(2, 0)
     k_along_z(2, (1, -1))
     got_k(0, 2)
-    k_along_x(2, (1, -1, 2))
+    k_along_x(2, (2, 1, -1))
     for dy in (1, 3, 2):
         got_q(dy, 1, 0)
         q_to_core(dy, 1)
@@ -282,9 +282,11 @@
     def send_k(dx, dz, dst, sem, device):
         out.go(kst.at[pl.ds(krow(dx, dz), ROWS)], dst, sem, device)
 
-    for c in (3, 1, 2, 0):
+    for c in (3, 2, 1, 0):
         dz = ZORDER[c]
-        terms = pair.grad_scores(c)
+        if c % 2 == 1:
+            pair.grad_scores(c // 2)
+        terms = pair.key_terms(c)
         kst[pl.ds(c * KC, KC)] = terms.astype(BF16)
         kp[dz] = terms[0:ROWS]
         if dz == 0:
@@ -320,9 +322,6 @@
             qst[slot] = core_sum(dy, dzl).astype(BF16)
             out.go(qst.at[slot], qyin.at[slot], qy_sem.at[slot], at.at_y(dy if dy < 3 else -1))
 
-    q_along_y_sums(1)
-    q_along_y_sums(0)
-
     def k_sum(dz):
         got(kx1.at[dz], kx1_sem.at[dz])
         got(kx1.at[4 + dz], kx1_sem.at[4 + dz])
@@ -332,9 +331,11 @@
         kst[pl.ds(krow(0, dz), ROWS)] = total.astype(BF16)
         send_k(0, dz, kzin.at[dz], kzin_sem.at[dz], at.at_zh(dz if dz < 3 else -1))
 
+    q_along_y_sums(1)
     total = k_sum(2)
     got(kx2.at[1], kx2_sem.at[1])
     k_send_z(2, total + kx2[1].astype(F32))
+    q_along_y_sums(0)
     for side in (0, 1):
         got(kzt.at[side], kzt_sem.at[side])
     kst[pl.ds(krow(2, 0), ROWS)] = (kp[4] + kzt[0].astype(F32) + kzt[1].astype(F32)).astype(BF16)
@@ -392,10 +393,13 @@
             sems(8), sems(2), sems(2), sems(4), sems(8), sems(8), sems(1),
         ],
         compiler_params=pltpu.CompilerParams(
-            collective_id=0, has_side_effects=True, vmem_limit_bytes=60 * 2**20
+            collective_id=0, has_side_effects=True, vmem_limit_bytes=44 * 2**20
         ),
         name="cycle_pairs",
-    )(queries, keys)
+    )(
+        pltpu.with_memory_space_constraint(queries, pltpu.HBM),
+        pltpu.with_memory_space_constraint(keys, pltpu.HBM),
+    )
 
 
 def solution(mesh):

time: 53.9 us -> 51.2 us (0.950)
  Pallas kernels: 50.9 us -> 49.2 us
  local copies, waits for them, and re-layouts: 2.28 us -> 1.32 us
    pallas_call x1, Pallas kernels: 50.9 us -> 49.2 us  [local(): pl.pallas_call(functools.partial(cycle_kernel, scale, frames), out_shape=...]
    unnamed x4 -> x2, local copies, waits for them, and re-layouts: 2.28 us -> 1.32 us
where the time goes in v5:
time: 51.2 us; the launch traced here: 51.1 us
  Pallas kernels  49.2 us (96%)
  local copies, waits for them, and re-layouts  1.32 us (3%)
  between operations  0.64 us (1%)
    pallas_call x1, Pallas kernels, local(): pl.pallas_call(functools.partial(cycle_kernel, scale, frames), out_shape=...  49.2 us
    unnamed x2, local copies, waits for them, and re-layouts  1.32 us

profile of v5, /device:TPU:1, one launch (start us, length us, event | category | flops | bytes accessed | tf_op | source)
XLA Modules:
  0.0 51.1 jit_solution(10290122706386671586)
XLA Ops:
  0.6 49.2 %cycle_pairs.1 = (f32[1,48,768]{2,1,0:T(8,128)S(1)}, f32[1,48,768]{2,1,0:T(8,128)S(1)}) custom-call(bf16[1,48,768]{2,1,0:T(8,128)(2,1)} %q_hbm.1, bf16[1,48,768]{2,1,0:T(8,128)(2,1)} %k_hbm.1), custom_call_target="tpu_custom_call" | custom-call | tf_op jit(solution)/shard_map/cycle_pairs/pallas_call | solution.py:382
  49.8 0.7 %copy.6 = f32[1,48,768]{2,1,0:T(8,128)} copy(f32[1,48,768]{2,1,0:T(8,128)S(1)} %get-tuple-element.4) | data formatting | bytes 294912
  50.5 0.7 %copy.7 = f32[1,48,768]{2,1,0:T(8,128)} copy(f32[1,48,768]{2,1,0:T(8,128)S(1)} %get-tuple-element.5) | data formatting | bytes 294912

commit v6 on v5

--- a/solution.py
+++ b/solution.py
@@ -91,15 +91,15 @@
 
 
 class Pair:
-    def __init__(self, scale, frames, qf, kf, st, bt, at, bh, ah, v, gr, gh, da, dv, ds, cmax, csum, cdel):
+    def __init__(self, scale, frames, qf, kf, st, bt, at, bh, ah, v, gr, gh, dv, ds, cmax, etop, csum, cdel):
         self.__dict__.update(locals())
 
-    def scores(self, c):
-        rows = pl.ds(c * KC, KC)
+    def scores(self, start, size):
+        rows = pl.ds(start, size)
         st = nt(self.kf[rows], self.qf[...]) * (self.scale * math.log2(math.e))
         self.st[rows] = st
         top = fold(st, jnp.max)
-        self.cmax[...] = top if c == 0 else jnp.maximum(self.cmax[...], top)
+        self.cmax[...] = top if start == 0 else jnp.maximum(self.cmax[...], top)
         e = jnp.exp2(st - jnp.max(st, axis=1, keepdims=True))
         b = e * (1.0 / jnp.sum(e, axis=1, keepdims=True))
         self.bt[rows] = b
@@ -107,49 +107,57 @@
         self.bh[rows] = bh
         self.v[rows] = nn(bh, self.qf[...]).astype(BF16)
 
-    def attend(self):
-        top = jnp.max(self.cmax[...], axis=0, keepdims=True)
+    def powers(self, start, size, top):
         total = jnp.zeros((8, TOK), F32)
-        for c in range(TOK // KC):
-            rows = pl.ds(c * KC, KC)
+        for first in range(start, start + size, KC):
+            rows = pl.ds(first, KC)
             e = jnp.exp2(self.st[rows] - top)
             self.at[rows] = e
             total = total + fold(e, jnp.sum)
-        inv = 1.0 / jnp.sum(total, axis=0, keepdims=True)
-        for c in range(TOK // KC):
-            rows = pl.ds(c * KC, KC)
-            a = self.at[rows] * inv
+        return total
+
+    def attend_early(self, size):
+        top = jnp.max(self.cmax[...], axis=0, keepdims=True)
+        self.etop[...] = jnp.broadcast_to(top, (8, TOK))
+        self.csum[...] = self.powers(0, size, top)
+
+    def attend(self, size):
+        top = jnp.max(self.cmax[...], axis=0, keepdims=True)
+        early = jnp.exp2(self.etop[0:1] - top)
+        late = self.powers(size, TOK - size, top)
+        total = jnp.sum(self.csum[...] * early + late, axis=0, keepdims=True)
+        inv = 1.0 / total
+        weight = early * inv
+        halves = jnp.zeros((8, TOK), F32)
+        for first in range(0, TOK, KC):
+            rows = pl.ds(first, KC)
+            a = self.at[rows] * (weight if first < size else inv)
             self.at[rows] = a
-            self.ah[rows] = a.astype(BF16)
+            ah = a.astype(BF16)
+            self.ah[rows] = ah
+            halves = halves + fold(ah.astype(F32), jnp.sum)
+        self.csum[...] = jnp.broadcast_to(jnp.sum(halves, axis=0, keepdims=True), (8, TOK))
 
     def residual(self, size=384):
         for c in range(TOK // size):
             rows = pl.ds(c * size, size)
             cycled = tn(self.ah[:, rows], self.v[...])
             g = (cycled - self.qf[rows].astype(F32)) * (1.0 / self.frames)
+            gh = g.astype(BF16)
             self.gr[rows] = g
-            self.gh[rows] = g.astype(BF16)
-
-    def grad_rows(self, size=384):
-        total = jnp.zeros((8, TOK), F32)
-        for c in range(TOK // size):
-            rows = pl.ds(c * size, size)
-            da = nt(self.v[rows], self.gh[...])
-            self.da[rows] = da
-            total = total + fold(da * self.at[rows], jnp.sum)
-        self.cdel[...] = jnp.broadcast_to(jnp.sum(total, axis=0, keepdims=True), (8, TOK))
-
-    def grad_warp(self, size=384):
-        for c in range(TOK // size):
-            rows = pl.ds(c * size, size)
-            self.dv[rows] = nn(self.ah[rows], self.gh[...]).astype(BF16)
-
-    def grad_scores(self, c, size=384):
-        rows = pl.ds(c * size, size)
-        db = nt(self.dv[rows], self.qf[...])
+            self.gh[rows] = gh
+            delta = jnp.sum(gh.astype(F32) * cycled, axis=1, keepdims=True)
+            self.cdel[:, rows] = jnp.broadcast_to(delta, (size, 128)).T[0:8] / self.csum[:, rows]
+
+    def grad_scores(self, start, size):
+        rows = pl.ds(start, size)
+        da = nt(self.v[rows], self.gh[...])
+        dv = nn(self.ah[rows], self.gh[...]).astype(BF16)
+        self.dv[rows] = dv
+        db = nt(dv, self.qf[...])
         b = self.bt[rows]
         delta = jnp.sum(db * b, axis=1, keepdims=True)
-        ds = self.at[rows] * (self.da[rows] - self.cdel[0:1]) + b * (db - delta)
+        ds = self.at[rows] * (da - self.cdel[0:1]) + b * (db - delta)
         self.ds[rows] = (ds * self.scale).astype(BF16)
 
     def key_terms(self, c, size=KC):
@@ -166,8 +174,8 @@
 
     return [
         whole(F32), whole(F32), whole(F32), whole(BF16), whole(BF16), whole(BF16),
-        whole(F32), whole(BF16), whole(F32), whole(BF16), whole(BF16),
-        pltpu.VMEM((8, TOK), F32), pltpu.VMEM((8, TOK), F32), pltpu.VMEM((8, TOK), F32),
+        whole(F32), whole(BF16), whole(BF16), whole(BF16),
+        *[pltpu.VMEM((8, TOK), F32)] * 4,
     ]
 
 
@@ -182,7 +190,7 @@
     return (((1 - dzl) * 2 + 1 - dc) * 4 + dy % 4) * ROWS
 
 
-def cycle_kernel(scale, frames, q_hbm, k_hbm, q_out, k_out, qf, kf, *scratch):
+def cycle_kernel(scale, frames, q_hbm, k_hbm, both, qf, kf, *scratch):
     pair = Pair(scale, frames, qf, kf, *scratch[:14])
     (
         kst, kp, kx1, kx2, kzt, kzin, qcst, qcin, qp, qst, qyin, qzst, qzin,
@@ -250,42 +258,44 @@
     got_q(0, 1, 0)
     q_along_y(1)
     q_to_core(0, 1)
+    for dy in (1, 3):
+        got_q(dy, 0, 0)
+        q_to_core(dy, 0)
+    got_k(2, 0)
+    k_along_z(2, (1, -1))
+    got_q(2, 0, 0)
+    q_to_core(2, 0)
     for dz in (1, 3):
         got_k(0, dz)
         k_along_x(dz, (1, -1))
     for dy in (1, 3, 2):
-        got_q(dy, 0, 0)
-        q_to_core(dy, 0)
-    got_k(2, 0)
-    k_along_z(2, (1, -1))
+        got_q(dy, 1, 0)
+        q_to_core(dy, 1)
     got_k(0, 2)
     k_along_x(2, (2, 1, -1))
-    for dy in (1, 3, 2):
-        got_q(dy, 1, 0)
-        q_to_core(dy, 1)
     for dzl in (0, 1):
         for dy in (0, 1, 3, 2):
             got_q(dy, dzl, 1)
 
     got_k(1, 0)
     got_k(3, 0)
-    for c, dz in enumerate(ZORDER):
-        if dz != 0:
-            for dx in (1, 3, 2):
-                got_k(dx, dz)
-        pair.scores(c)
-    pair.attend()
+    pair.scores(0, KC)
+    for dz in (1, 3):
+        for dx in (1, 3, 2):
+            got_k(dx, dz)
+    pair.scores(KC, 2 * KC)
+    pair.attend_early(3 * KC)
+    for dx in (1, 3, 2):
+        got_k(dx, 2)
+    pair.scores(3 * KC, KC)
+    pair.attend(3 * KC)
     pair.residual()
-    pair.grad_rows()
-    pair.grad_warp()
 
     def send_k(dx, dz, dst, sem, device):
         out.go(kst.at[pl.ds(krow(dx, dz), ROWS)], dst, sem, device)
 
-    for c in (3, 2, 1, 0):
-        dz = ZORDER[c]
-        if c % 2 == 1:
-            pair.grad_scores(c // 2)
+    def key_terms(dz):
+        c = ZORDER.index(dz)
         terms = pair.key_terms(c)
         kst[pl.ds(c * KC, KC)] = terms.astype(BF16)
         kp[dz] = terms[0:ROWS]
@@ -300,7 +310,7 @@
         send_k(1, dz, kx1.at[dz], kx1_sem.at[dz], at.at_x(1))
         send_k(3, dz, kx1.at[4 + dz], kx1_sem.at[4 + dz], at.at_x(-1))
 
-    for dzl in (1, 0):
+    def query_terms(dzl):
         terms = pair.query_terms(1 - dzl)
         rows = pl.ds(dzl * KC, KC)
         qcst[rows] = terms[0:KC].astype(BF16)
@@ -310,6 +320,15 @@
             block = pl.ds(slot * ROWS, ROWS)
             out.go(qcst.at[block], qcin.at[block], qc_sem.at[slot], at.at_core())
 
+    pair.grad_scores(3 * KC, KC)
+    key_terms(2)
+    pair.grad_scores(0, 3 * KC)
+    key_terms(1)
+    key_terms(3)
+    query_terms(1)
+    key_terms(0)
+    query_terms(0)
+
     def core_sum(dy, dzl):
         slot = dzl * 4 + dy
         block = pl.ds(slot * ROWS, ROWS)
@@ -331,17 +350,17 @@
         kst[pl.ds(krow(0, dz), ROWS)] = total.astype(BF16)
         send_k(0, dz, kzin.at[dz], kzin_sem.at[dz], at.at_zh(dz if dz < 3 else -1))
 
-    q_along_y_sums(1)
     total = k_sum(2)
     got(kx2.at[1], kx2_sem.at[1])
     k_send_z(2, total + kx2[1].astype(F32))
+    q_along_y_sums(1)
+    k_send_z(3, k_sum(3))
     q_along_y_sums(0)
+    k_send_z(1, k_sum(1))
     for side in (0, 1):
         got(kzt.at[side], kzt_sem.at[side])
     kst[pl.ds(krow(2, 0), ROWS)] = (kp[4] + kzt[0].astype(F32) + kzt[1].astype(F32)).astype(BF16)
     send_k(2, 0, kx2.at[0], kx2_sem.at[0], at.at_x(2))
-    for dz in (1, 3):
-        k_send_z(dz, k_sum(dz))
 
     def y_sum(dzl):
         total = core_sum(0, dzl)
@@ -358,11 +377,11 @@
     got(kx2.at[0], kx2_sem.at[0])
     total = total + kx2[0].astype(F32)
     got(qzin, qz_sem.at[0])
-    q_out[0] = q_total + qzin[...].astype(F32)
+    both[0] = q_total + qzin[...].astype(F32)
     for dz in (1, 3, 2):
         got(kzin.at[dz], kzin_sem.at[dz])
         total = total + kzin[dz].astype(F32)
-    k_out[0] = total
+    both[1] = total
     out.finish()
 
 
@@ -379,11 +398,11 @@
     def sems(count):
         return pltpu.SemaphoreType.DMA((count,))
 
-    return pl.pallas_call(
+    both = pl.pallas_call(
         functools.partial(cycle_kernel, scale, frames),
-        out_shape=(own, own),
+        out_shape=jax.ShapeDtypeStruct((2, ROWS, TOK), F32),
         in_specs=[hbm, hbm],
-        out_specs=(vmem, vmem),
+        out_specs=vmem,
         scratch_shapes=[
             buf(TOK), buf(TOK),
             *pair_scratch(),
@@ -400,6 +419,7 @@
         pltpu.with_memory_space_constraint(queries, pltpu.HBM),
         pltpu.with_memory_space_constraint(keys, pltpu.HBM),
     )
+    return (both[0:1], both[1:2])
 
 
 def solution(mesh):

time: 51.2 us -> 49.5 us (0.967); the launches traced: 51.1 us -> 48.9 us
  Pallas kernels: 49.2 us -> 47.5 us
  local copies, waits for them, and re-layouts: 1.32 us -> 0.73 us
    pallas_call x1, Pallas kernels: 49.2 us -> 47.5 us  [local(): pl.pallas_call(functools.partial(cycle_kernel, scale, frames), out_shape=...]
    unnamed x2 -> x0, local copies, waits for them, and re-layouts: 1.32 us -> none
    slice x0 -> x1, local copies, waits for them, and re-layouts: none -> 0.73 us  [local(): return (both[0:1], both[1:2])]
where the time goes in v6:
time: 49.5 us; the launch traced here: 48.9 us
  Pallas kernels  47.5 us (96%)
  local copies, waits for them, and re-layouts  0.73 us (1%)
  between operations  0.64 us (1%)
    pallas_call x1, Pallas kernels, local(): pl.pallas_call(functools.partial(cycle_kernel, scale, frames), out_shape=...  47.5 us

profile of v6, /device:TPU:1, one launch (start us, length us, event | category | flops | bytes accessed | tf_op | source)
XLA Modules:
  0.0 48.9 jit_solution(1427976888161124994)
XLA Ops:
  0.6 47.5 %cycle_pairs.1 = f32[2,48,768]{2,1,0:T(8,128)S(1)} custom-call(bf16[1,48,768]{2,1,0:T(8,128)(2,1)} %q_hbm.1, bf16[1,48,768]{2,1,0:T(8,128)(2,1)} %k_hbm.1), custom_call_target="tpu_custom_call" | custom-call | tf_op jit(solution)/shard_map/cycle_pairs/pallas_call | solution.py:401
  48.2 0.7 %fusion = (f32[1,48,768]{2,1,0:T(8,128)}, f32[1,48,768]{2,1,0:T(8,128)}) fusion(f32[2,48,768]{2,1,0:T(8,128)S(1)} %cycle_pairs.1), kind=kLoop, calls=%fused_computation | loop fusion | bytes 589824 | tf_op jit(solution)/shard_map/slice | solution.py:422

commit v7 on v6

--- a/solution.py
+++ b/solution.py
@@ -180,6 +180,9 @@
 
 
 ZORDER = (0, 1, 3, 2)
+
+
+PIECES = ((0, 32), (32, 16))
 
 
 def krow(dx, dz):
@@ -306,7 +309,15 @@
         if dz == 3:
             send_k(2, 3, kzt.at[1], kzt_sem.at[1], at.at_zh(-1))
         if dz == 2:
-            send_k(2, 2, kx2.at[1], kx2_sem.at[1], at.at_x(2))
+            for part, (first, count) in enumerate(PIECES):
+                rows = pl.ds(first, count)
+                for dx, dst, sem, device in (
+                    (2, kx2.at[1, rows], kx2_sem.at[1 + part], at.at_x(2)),
+                    (1, kx1.at[2, rows], kx1_sem.at[2 + 6 * part], at.at_x(1)),
+                    (3, kx1.at[6, rows], kx1_sem.at[6 + 3 * part], at.at_x(-1)),
+                ):
+                    out.go(kst.at[pl.ds(krow(dx, 2) + first, count)], dst, sem, device)
+            return
         send_k(1, dz, kx1.at[dz], kx1_sem.at[dz], at.at_x(1))
         send_k(3, dz, kx1.at[4 + dz], kx1_sem.at[4 + dz], at.at_x(-1))
 
@@ -339,7 +350,14 @@
         for dy in (2, 1, 3):
             slot = dzl * 4 + dy
             qst[slot] = core_sum(dy, dzl).astype(BF16)
-            out.go(qst.at[slot], qyin.at[slot], qy_sem.at[slot], at.at_y(dy if dy < 3 else -1))
+            if dzl == 0:
+                out.go(qst.at[slot], qyin.at[slot], qy_sem.at[slot], at.at_y(dy if dy < 3 else -1))
+        if dzl == 1:
+            for part, (first, count) in enumerate(PIECES):
+                for dy in (2, 1, 3):
+                    block = (4 + dy, pl.ds(first, count))
+                    sem = qy_sem.at[4 + 4 * part + dy]
+                    out.go(qst.at[block], qyin.at[block], sem, at.at_y(dy if dy < 3 else -1))
 
     def k_sum(dz):
         got(kx1.at[dz], kx1_sem.at[dz])
@@ -350,9 +368,15 @@
         kst[pl.ds(krow(0, dz), ROWS)] = total.astype(BF16)
         send_k(0, dz, kzin.at[dz], kzin_sem.at[dz], at.at_zh(dz if dz < 3 else -1))
 
-    total = k_sum(2)
-    got(kx2.at[1], kx2_sem.at[1])
-    k_send_z(2, total + kx2[1].astype(F32))
+    for part, (first, count) in enumerate(PIECES):
+        rows = pl.ds(first, count)
+        got(kx2.at[1, rows], kx2_sem.at[1 + part])
+        got(kx1.at[2, rows], kx1_sem.at[2 + 6 * part])
+        got(kx1.at[6, rows], kx1_sem.at[6 + 3 * part])
+        total = kp[2, rows] + kx1[2, rows].astype(F32) + kx1[6, rows].astype(F32)
+        block = pl.ds(krow(0, 2) + first, count)
+        kst[block] = (total + kx2[1, rows].astype(F32)).astype(BF16)
+        out.go(kst.at[block], kzin.at[2, rows], kzin_sem.at[2 + 2 * part], at.at_zh(2))
     q_along_y_sums(1)
     k_send_z(3, k_sum(3))
     q_along_y_sums(0)
@@ -362,24 +386,31 @@
     kst[pl.ds(krow(2, 0), ROWS)] = (kp[4] + kzt[0].astype(F32) + kzt[1].astype(F32)).astype(BF16)
     send_k(2, 0, kx2.at[0], kx2_sem.at[0], at.at_x(2))
 
-    def y_sum(dzl):
-        total = core_sum(0, dzl)
+    own = core_sum(0, 1)
+    for part, (first, count) in enumerate(PIECES):
+        rows = pl.ds(first, count)
+        total = own[first : first + count]
         for dy in (1, 3, 2):
-            slot = dzl * 4 + dy
-            got(qyin.at[slot], qy_sem.at[slot])
-            total = total + qyin[slot].astype(F32)
-        return total
-
-    qzst[...] = y_sum(1).astype(BF16)
-    out.go(qzst, qzin, qz_sem.at[0], at.at_zl())
-    q_total = y_sum(0)
+            got(qyin.at[4 + dy, rows], qy_sem.at[4 + 4 * part + dy])
+            total = total + qyin[4 + dy, rows].astype(F32)
+        qzst[rows] = total.astype(BF16)
+        out.go(qzst.at[rows], qzin.at[rows], qz_sem.at[part], at.at_zl())
+    q_total = core_sum(0, 0)
+    for dy in (1, 3, 2):
+        got(qyin.at[dy], qy_sem.at[dy])
+        q_total = q_total + qyin[dy].astype(F32)
     total = k_sum(0)
     got(kx2.at[0], kx2_sem.at[0])
     total = total + kx2[0].astype(F32)
-    got(qzin, qz_sem.at[0])
+    for part, (first, count) in enumerate(PIECES):
+        got(qzin.at[pl.ds(first, count)], qz_sem.at[part])
     both[0] = q_total + qzin[...].astype(F32)
     for dz in (1, 3, 2):
-        got(kzin.at[dz], kzin_sem.at[dz])
+        if dz == 2:
+            for part, (first, count) in enumerate(PIECES):
+                got(kzin.at[2, pl.ds(first, count)], kzin_sem.at[2 + 2 * part])
+        else:
+            got(kzin.at[dz], kzin_sem.at[dz])
         total = total + kzin[dz].astype(F32)
     both[1] = total
     out.finish()
@@ -408,8 +439,8 @@
             *pair_scratch(),
             buf(TOK), buf(5, ROWS, dtype=F32), buf(8, ROWS), buf(2, ROWS), buf(2, ROWS), buf(4, ROWS),
             buf(8 * ROWS), buf(8 * ROWS), buf(8 * ROWS, dtype=F32), buf(8, ROWS), buf(8, ROWS), buf(ROWS), buf(ROWS),
-            sems(2), sems(60), sems(16), sems(16),
-            sems(8), sems(2), sems(2), sems(4), sems(8), sems(8), sems(1),
+            sems(2), sems(68), sems(16), sems(16),
+            sems(10), sems(3), sems(2), sems(5), sems(8), sems(12), sems(2),
         ],
         compiler_params=pltpu.CompilerParams(
             collective_id=0, has_side_effects=True, vmem_limit_bytes=44 * 2**20

time: 49.5 us -> 49.1 us (level)
  no operation moved by 1% of the time
where the time goes in v7:
time: 49.1 us; the launch traced here: 48.6 us
  Pallas kernels  47.3 us (96%)
  local copies, waits for them, and re-layouts  0.73 us (1%)
  between operations  0.64 us (1%)
    pallas_call x1, Pallas kernels, local(): pl.pallas_call(functools.partial(cycle_kernel, scale, frames), out_shape=...  47.3 us

profile of v7, /device:TPU:1, one launch (start us, length us, event | category | flops | bytes accessed | tf_op | source)
XLA Modules:
  0.0 48.6 jit_solution(17511275260075319650)
XLA Ops:
  0.6 47.3 %cycle_pairs.1 = f32[2,48,768]{2,1,0:T(8,128)S(1)} custom-call(bf16[1,48,768]{2,1,0:T(8,128)(2,1)} %q_hbm.1, bf16[1,48,768]{2,1,0:T(8,128)(2,1)} %k_hbm.1), custom_call_target="tpu_custom_call" | custom-call | tf_op jit(solution)/shard_map/cycle_pairs/pallas_call | solution.py:432
  47.9 0.7 %fusion = (f32[1,48,768]{2,1,0:T(8,128)}, f32[1,48,768]{2,1,0:T(8,128)}) fusion(f32[2,48,768]{2,1,0:T(8,128)S(1)} %cycle_pairs.1), kind=kLoop, calls=%fused_computation | loop fusion | bytes 589824 | tf_op jit(solution)/shard_map/slice | solution.py:453

commit v8 on v7

--- a/solution.py
+++ b/solution.py
@@ -240,6 +240,13 @@
         for step in steps:
             out.go(kblock(0, dz), kblock(-step, dz), ksem(-step, dz), at.at_x(step))
 
+    def far_piece(dx, part):
+        first, count = PIECES[part]
+        return kf.at[pl.ds(krow(dx, 2) + first, count)]
+
+    def far_sem(dx, part):
+        return k_sem.at[krow(dx, 2) // ROWS + 4 * part]
+
     def k_along_z(dx, steps):
         for step in steps:
             out.go(kblock(dx, 0), kblock(dx, -step), ksem(dx, -step), at.at_zh(step))
@@ -255,7 +262,9 @@
     k_along_z(0, (1, -1))
     k_along_x(0, (2, 1, -1))
     q_along_y(0)
-    k_along_z(0, (2,))
+    for part, (first, count) in enumerate(PIECES):
+        src = kf.at[pl.ds(krow(0, 0) + first, count)]
+        out.go(src, far_piece(0, part), far_sem(0, part), at.at_zh(2))
     q_to_core(0, 0)
 
     got_q(0, 1, 0)
@@ -274,8 +283,11 @@
     for dy in (1, 3, 2):
         got_q(dy, 1, 0)
         q_to_core(dy, 1)
-    got_k(0, 2)
-    k_along_x(2, (2, 1, -1))
+    for part in (0, 1):
+        got(far_piece(0, part), far_sem(0, part))
+        for step in (2, 1, -1):
+            dx = -step % 4
+            out.go(far_piece(0, part), far_piece(dx, part), far_sem(dx, part), at.at_x(step))
     for dzl in (0, 1):
         for dy in (0, 1, 3, 2):
             got_q(dy, dzl, 1)
@@ -289,7 +301,8 @@
     pair.scores(KC, 2 * KC)
     pair.attend_early(3 * KC)
     for dx in (1, 3, 2):
-        got_k(dx, 2)
+        for part in (0, 1):
+            got(far_piece(dx, part), far_sem(dx, part))
     pair.scores(3 * KC, KC)
     pair.attend(3 * KC)
     pair.residual()
@@ -439,7 +452,7 @@
             *pair_scratch(),
             buf(TOK), buf(5, ROWS, dtype=F32), buf(8, ROWS), buf(2, ROWS), buf(2, ROWS), buf(4, ROWS),
             buf(8 * ROWS), buf(8 * ROWS), buf(8 * ROWS, dtype=F32), buf(8, ROWS), buf(8, ROWS), buf(ROWS), buf(ROWS),
-            sems(2), sems(68), sems(16), sems(16),
+            sems(2), sems(72), sems(16), sems(20),
             sems(10), sems(3), sems(2), sems(5), sems(8), sems(12), sems(2),
         ],
         compiler_params=pltpu.CompilerParams(

time: 49.1 us -> 48.4 us (0.986)
  no operation moved by 1% of the time
where the time goes in v8:
time: 48.4 us
  Pallas kernels  47 us (97%)
  local copies, waits for them, and re-layouts  0.73 us (2%)
  between operations  0.64 us (1%)
    pallas_call x1, Pallas kernels, local(): pl.pallas_call(functools.partial(cycle_kernel, scale, frames), out_shape=...  47 us

profile of v8, /device:TPU:1, one launch (start us, length us, event | category | flops | bytes accessed | tf_op | source)
XLA Modules:
  0.0 48.4 jit_solution(7027830402165052241)
XLA Ops:
  0.6 47.0 %cycle_pairs.1 = f32[2,48,768]{2,1,0:T(8,128)S(1)} custom-call(bf16[1,48,768]{2,1,0:T(8,128)(2,1)} %q_hbm.1, bf16[1,48,768]{2,1,0:T(8,128)(2,1)} %k_hbm.1), custom_call_target="tpu_custom_call" | custom-call | tf_op jit(solution)/shard_map/cycle_pairs/pallas_call | solution.py:445
  47.6 0.7 %fusion = (f32[1,48,768]{2,1,0:T(8,128)}, f32[1,48,768]{2,1,0:T(8,128)}) fusion(f32[2,48,768]{2,1,0:T(8,128)S(1)} %cycle_pairs.1), kind=kLoop, calls=%fused_computation | loop fusion | bytes 589824 | tf_op jit(solution)/shard_map/slice | solution.py:466

commit v9 on v8

--- a/solution.py
+++ b/solution.py
@@ -260,7 +260,7 @@
 
     out.go(qblock(0, 0, 0), qblock(0, 1, 0), qsem(0, 1, 0), at.at_zl())
     k_along_z(0, (1, -1))
-    k_along_x(0, (2, 1, -1))
+    k_along_x(0, (1, -1, 2))
     q_along_y(0)
     for part, (first, count) in enumerate(PIECES):
         src = kf.at[pl.ds(krow(0, 0) + first, count)]

time: 48.4 us -> 48.7 us (level)
  no operation moved by 1% of the time
where the time goes in v9:
time: 48.7 us; the launch traced here: 48.6 us
  Pallas kernels  47.2 us (97%)
  local copies, waits for them, and re-layouts  0.73 us (1%)
  between operations  0.64 us (1%)
    pallas_call x1, Pallas kernels, local(): pl.pallas_call(functools.partial(cycle_kernel, scale, frames), out_shape=...  47.2 us

profile of v9, /device:TPU:1, one launch (start us, length us, event | category | flops | bytes accessed | tf_op | source)
XLA Modules:
  0.0 48.6 jit_solution(2153329222236099856)
XLA Ops:
  0.6 47.2 %cycle_pairs.1 = f32[2,48,768]{2,1,0:T(8,128)S(1)} custom-call(bf16[1,48,768]{2,1,0:T(8,128)(2,1)} %q_hbm.1, bf16[1,48,768]{2,1,0:T(8,128)(2,1)} %k_hbm.1), custom_call_target="tpu_custom_call" | custom-call | tf_op jit(solution)/shard_map/cycle_pairs/pallas_call | solution.py:445
  47.9 0.7 %fusion = (f32[1,48,768]{2,1,0:T(8,128)}, f32[1,48,768]{2,1,0:T(8,128)}) fusion(f32[2,48,768]{2,1,0:T(8,128)S(1)} %cycle_pairs.1), kind=kLoop, calls=%fused_computation | loop fusion | bytes 589824 | tf_op jit(solution)/shard_map/slice | solution.py:466
